TPU v7x, 512 devices: a whole 4x8x8 slice. The times are simulated.
512 devices in a mesh: section: 16 (over y, core), dom: 32 (over z, x).
Axes of the slice: x: 4, y: 8, z: 8, core: 2. Of those that a mesh axis runs over, the one named last changes fastest.
Arguments:
- right_sides: float32 [4096, 32, 128], P(('section', 'dom')), may hold values from -6 to 6
- diag_inverse: bfloat16 [4096, 128, 128], P(('section', 'dom')), as said below
- diag_blocks: bfloat16 [4096, 128, 128], P(('section', 'dom')), as said below
- lower_blocks: bfloat16 [4096, 3, 128, 128], P(('section', 'dom'))
- upper_blocks: bfloat16 [4096, 3, 128, 128], P(('section', 'dom'))
- halo_blocks: bfloat16 [4096, 2, 128, 128], P(('section', 'dom')), may hold values from -0.1875 to 0.1875
- lower_index: int32 [4096, 3], P(('section', 'dom')), may hold values from 0 to 7, as said below
- upper_index: int32 [4096, 3], P(('section', 'dom')), may hold values from 0 to 7, as said below
- halo_index: int32 [4096, 2], P(('section', 'dom')), may hold values from 0 to 7, as said below
Outputs:
- solution: float32 [4096, 32, 128], P(('section', 'dom'))
- product: float32 [4096, 32, 128], P(('section', 'dom'))
Inputs may be any that keep to these rules, and one draw needn't show every extreme that they name: `lower_index`: for block row g with k = g mod 8, every entry lies in 0 to k, and the first entry equals k. `upper_index`: for block row g with k = g mod 8, every entry lies in k to 7, and the first entry equals k. `halo_index`: for block row g the first entry equals g mod 8. `diag_inverse`: each block is the identity scaled row by row plus a full block. `diag_blocks`: each block is the identity scaled row by row plus a full block.
All inputs are finite; a program needn't handle non-finite values.
Results may differ from a plain program's by a relative error of at most 0.029.
Values may be sent and summed in bfloat16 or wider, within the bound.
A program may use at most 64 MiB of HBM per device.

v0:
```python
import jax
import jax.numpy as jnp
from jax import lax
from jax.sharding import PartitionSpec as P

RIM = 4


def shifted(value, axis, steps):
    count = lax.axis_size(axis)
    first, last = (max(0, -steps), min(count, count - steps))
    return lax.ppermute(value, axis, [(source, source + steps) for source in range(first, last)])


def extended(block, sides, width):
    for axis, dim in sides:
        count = lax.axis_size(axis)
        forward = [(i, i + 1) for i in range(count - 1)]
        backward = [(target, source) for source, target in forward]
        low = lax.ppermute(
            lax.slice_in_dim(block, block.shape[dim] - width, None, axis=dim), axis, forward
        )
        high = lax.ppermute(lax.slice_in_dim(block, 0, width, axis=dim), axis, backward)
        block = jnp.concatenate([low, block, high], axis=dim)
    return block


def select_rows(pointers, first, candidates):
    offsets = jnp.arange(candidates.shape[0], dtype=jnp.int32) + first
    weights = (pointers[:, None] == offsets[None, :]).astype(jnp.bfloat16)
    picked = jnp.einsum("sr,rqb->sqb", weights, candidates, preferred_element_type=jnp.float32)
    return picked.astype(jnp.bfloat16)


def solve_down(target, inverse, lower_part, pointers, inflow):
    solved_rows = []
    narrow_rows = []
    inflow_narrow = inflow.astype(jnp.bfloat16)
    for position in range(target.shape[0]):
        candidates = jnp.stack(narrow_rows + [inflow_narrow], axis=0)
        source = select_rows(pointers[position], 0, candidates)
        summed = jnp.einsum(
            "sqb,sbc->qc", source, lower_part[position], preferred_element_type=jnp.float32
        )
        gap = (target[position] - summed).astype(jnp.bfloat16)
        result = jnp.dot(gap, inverse[position], preferred_element_type=jnp.float32)
        solved_rows.append(result)
        narrow_rows.append(result.astype(jnp.bfloat16))
    return jnp.stack(solved_rows, axis=0)


def solve_up(target, inverse, upper_part, pointers, inflow):
    count = target.shape[0]
    solved_rows = []
    narrow_rows = []
    inflow_narrow = inflow.astype(jnp.bfloat16)
    for position in range(count - 1, -1, -1):
        candidates = jnp.stack([inflow_narrow] + narrow_rows, axis=0)
        source = select_rows(pointers[position], position, candidates)
        summed = jnp.einsum(
            "sqb,sbc->qc", source, upper_part[position], preferred_element_type=jnp.float32
        )
        result = target[position] - jnp.dot(
            summed.astype(jnp.bfloat16), inverse[position], preferred_element_type=jnp.float32
        )
        solved_rows.insert(0, result)
        narrow_rows.insert(0, result.astype(jnp.bfloat16))
    return jnp.stack(solved_rows, axis=0)


def apply_rows(
    rounded,
    diag_part,
    lower_part,
    lower_pointers,
    upper_part,
    upper_pointers,
    halo_part,
    halo_pointers,
    before,
    after,
    rim_rows,
):
    positions = jnp.arange(rounded.shape[0], dtype=jnp.int32)[:, None]
    lower_source = jnp.where(
        (lower_pointers == positions)[:, :, None, None],
        before[None, None],
        jnp.take(rounded, lower_pointers, axis=0),
    )
    upper_source = jnp.where(
        (upper_pointers == positions)[:, :, None, None],
        after[None, None],
        jnp.take(rounded, upper_pointers, axis=0),
    )
    halo_source = jnp.take(rim_rows, halo_pointers, axis=0)
    total = jnp.einsum("rqb,rbc->rqc", rounded, diag_part, preferred_element_type=jnp.float32)
    total = total + jnp.einsum(
        "rsqb,rsbc->rqc", lower_source, lower_part, preferred_element_type=jnp.float32
    )
    total = total + jnp.einsum(
        "rsqb,rsbc->rqc", upper_source, upper_part, preferred_element_type=jnp.float32
    )
    total = total + jnp.einsum(
        "rsqb,rsbc->rqc", halo_source, halo_part, preferred_element_type=jnp.float32
    )
    return total


def on_device(
    right_sides,
    diag_inverse,
    diag_blocks,
    lower_blocks,
    upper_blocks,
    halo_blocks,
    lower_index,
    upper_index,
    halo_index,
):
    count_rhs = right_sides.shape[1]
    width = right_sides.shape[2]
    inflow_zero = jnp.zeros((count_rhs, width), jnp.float32)
    section_count = lax.axis_size("section")

    def forward_turn(turn_index, inflow):
        solved = solve_down(right_sides, diag_inverse, lower_blocks, lower_index, inflow)
        return shifted(solved[-1], "section", 1)

    inflow = lax.fori_loop(0, section_count - 1, forward_turn, inflow_zero)
    forward = solve_down(right_sides, diag_inverse, lower_blocks, lower_index, inflow)

    def backward_turn(turn_index, inflow):
        solved = solve_up(forward, diag_inverse, upper_blocks, upper_index, inflow)
        return shifted(solved[0], "section", -1)

    outflow = lax.fori_loop(0, section_count - 1, backward_turn, inflow_zero)
    solution = solve_up(forward, diag_inverse, upper_blocks, upper_index, outflow)
    rounded = solution.astype(jnp.bfloat16)
    padded = extended(rounded, (("section", 0),), 1)
    widened = extended(rounded, (("dom", 0),), RIM)
    rim_rows = jnp.concatenate([widened[:RIM], widened[widened.shape[0] - RIM :]], axis=0)
    product = apply_rows(
        rounded,
        diag_blocks,
        lower_blocks,
        lower_index,
        upper_blocks,
        upper_index,
        halo_blocks,
        halo_index,
        padded[0],
        padded[-1],
        rim_rows,
    )
    return (solution, product)


def solution(mesh):
    in_specs = (
        P(("section", "dom"), None, None),
        P(("section", "dom"), None, None),
        P(("section", "dom"), None, None),
        P(("section", "dom"), None, None, None),
        P(("section", "dom"), None, None, None),
        P(("section", "dom"), None, None, None),
        P(("section", "dom"), None),
        P(("section", "dom"), None),
        P(("section", "dom"), None),
    )
    out_specs = (P(("section", "dom"), None, None), P(("section", "dom"), None, None))
    return jax.shard_map(
        on_device, mesh=mesh, in_specs=in_specs, out_specs=out_specs, check_vma=False
    )
```

profile of v0, /device:TPU:281, one launch (start us, length us, event | category | flops | bytes accessed | tf_op | source)
XLA Modules:
  0.0 391.5 jit_solution(17528457309569890415)
XLA Ops:
  2.8 203.2 %while.20 = (s32[]{:T(128)}, bf16[32,128]{1,0:T(8,128)(2,1)S(1)}, f32[8,32,128]{2,1,0:T(8,128)}, s32[8,3]{1,0:T(8,128)S(1)}, bf16[8,3,128,128]{3,2,1,0:T(8,128)(2,1)}, /*index=5*/bf16[8,128,128]{2,1,0:T(8,128)(2,1)}, s32[]{:T(128)}) while((s32[]{:T(128)}, bf16[32,128]{1,0:T(8,128)(2,1)S(1)}, f32[8,32,128]{2,1,0:T(8,128)}, ...), condition=%wide.region_1.0_spmd, body=%wide.region_0.0_spmd.sunk | while | flops 34619500 | bytes 7086569 | solution.py:129
  10.3 5.0 %collective-permute-start = (bf16[32,128]{1,0:T(8,128)(2,1)S(1)}, bf16[32,128]{1,0:T(8,128)(2,1)S(1)}, u32[]{:S(2)}, u32[]{:S(2)}) collective-permute-start(bf16[32,128]{1,0:T(8,128)(2,1)S(1)} %fusion.641), channel_id=1, source_target_pairs={{0,32},{32,64},{64,96},{96,128},{128,160},{160,192},{192,224},{224... | collective-permute-start | bytes 24584 | tf_op jit(solution)/shard_map/while/body/eval_jaxpr/ppermute | solution.py:12
  23.4 5.4 %collective-permute-start = (bf16[32,128]{1,0:T(8,128)(2,1)S(1)}, bf16[32,128]{1,0:T(8,128)(2,1)S(1)}, u32[]{:S(2)}, u32[]{:S(2)}) collective-permute-start(bf16[32,128]{1,0:T(8,128)(2,1)S(1)} %fusion.641), channel_id=1, source_target_pairs={{0,32},{32,64},{64,96},{96,128},{128,160},{160,192},{192,224},{224... | collective-permute-start | bytes 24584 | tf_op jit(solution)/shard_map/while/body/eval_jaxpr/ppermute | solution.py:12
  37.0 5.4 %collective-permute-start = (bf16[32,128]{1,0:T(8,128)(2,1)S(1)}, bf16[32,128]{1,0:T(8,128)(2,1)S(1)}, u32[]{:S(2)}, u32[]{:S(2)}) collective-permute-start(bf16[32,128]{1,0:T(8,128)(2,1)S(1)} %fusion.641), channel_id=1, source_target_pairs={{0,32},{32,64},{64,96},{96,128},{128,160},{160,192},{192,224},{224... | collective-permute-start | bytes 24584 | tf_op jit(solution)/shard_map/while/body/eval_jaxpr/ppermute | solution.py:12
  50.6 5.4 %collective-permute-start = (bf16[32,128]{1,0:T(8,128)(2,1)S(1)}, bf16[32,128]{1,0:T(8,128)(2,1)S(1)}, u32[]{:S(2)}, u32[]{:S(2)}) collective-permute-start(bf16[32,128]{1,0:T(8,128)(2,1)S(1)} %fusion.641), channel_id=1, source_target_pairs={{0,32},{32,64},{64,96},{96,128},{128,160},{160,192},{192,224},{224... | collective-permute-start | bytes 24584 | tf_op jit(solution)/shard_map/while/body/eval_jaxpr/ppermute | solution.py:12
  64.1 5.4 %collective-permute-start = (bf16[32,128]{1,0:T(8,128)(2,1)S(1)}, bf16[32,128]{1,0:T(8,128)(2,1)S(1)}, u32[]{:S(2)}, u32[]{:S(2)}) collective-permute-start(bf16[32,128]{1,0:T(8,128)(2,1)S(1)} %fusion.641), channel_id=1, source_target_pairs={{0,32},{32,64},{64,96},{96,128},{128,160},{160,192},{192,224},{224... | collective-permute-start | bytes 24584 | tf_op jit(solution)/shard_map/while/body/eval_jaxpr/ppermute | solution.py:12
  77.7 5.4 %collective-permute-start = (bf16[32,128]{1,0:T(8,128)(2,1)S(1)}, bf16[32,128]{1,0:T(8,128)(2,1)S(1)}, u32[]{:S(2)}, u32[]{:S(2)}) collective-permute-start(bf16[32,128]{1,0:T(8,128)(2,1)S(1)} %fusion.641), channel_id=1, source_target_pairs={{0,32},{32,64},{64,96},{96,128},{128,160},{160,192},{192,224},{224... | collective-permute-start | bytes 24584 | tf_op jit(solution)/shard_map/while/body/eval_jaxpr/ppermute | solution.py:12
  91.3 5.4 %collective-permute-start = (bf16[32,128]{1,0:T(8,128)(2,1)S(1)}, bf16[32,128]{1,0:T(8,128)(2,1)S(1)}, u32[]{:S(2)}, u32[]{:S(2)}) collective-permute-start(bf16[32,128]{1,0:T(8,128)(2,1)S(1)} %fusion.641), channel_id=1, source_target_pairs={{0,32},{32,64},{64,96},{96,128},{128,160},{160,192},{192,224},{224... | collective-permute-start | bytes 24584 | tf_op jit(solution)/shard_map/while/body/eval_jaxpr/ppermute | solution.py:12
  104.9 5.4 %collective-permute-start = (bf16[32,128]{1,0:T(8,128)(2,1)S(1)}, bf16[32,128]{1,0:T(8,128)(2,1)S(1)}, u32[]{:S(2)}, u32[]{:S(2)}) collective-permute-start(bf16[32,128]{1,0:T(8,128)(2,1)S(1)} %fusion.641), channel_id=1, source_target_pairs={{0,32},{32,64},{64,96},{96,128},{128,160},{160,192},{192,224},{224... | collective-permute-start | bytes 24584 | tf_op jit(solution)/shard_map/while/body/eval_jaxpr/ppermute | solution.py:12
  118.4 5.4 %collective-permute-start = (bf16[32,128]{1,0:T(8,128)(2,1)S(1)}, bf16[32,128]{1,0:T(8,128)(2,1)S(1)}, u32[]{:S(2)}, u32[]{:S(2)}) collective-permute-start(bf16[32,128]{1,0:T(8,128)(2,1)S(1)} %fusion.641), channel_id=1, source_target_pairs={{0,32},{32,64},{64,96},{96,128},{128,160},{160,192},{192,224},{224... | collective-permute-start | bytes 24584 | tf_op jit(solution)/shard_map/while/body/eval_jaxpr/ppermute | solution.py:12
  132.0 5.4 %collective-permute-start = (bf16[32,128]{1,0:T(8,128)(2,1)S(1)}, bf16[32,128]{1,0:T(8,128)(2,1)S(1)}, u32[]{:S(2)}, u32[]{:S(2)}) collective-permute-start(bf16[32,128]{1,0:T(8,128)(2,1)S(1)} %fusion.641), channel_id=1, source_target_pairs={{0,32},{32,64},{64,96},{96,128},{128,160},{160,192},{192,224},{224... | collective-permute-start | bytes 24584 | tf_op jit(solution)/shard_map/while/body/eval_jaxpr/ppermute | solution.py:12
  145.6 5.4 %collective-permute-start = (bf16[32,128]{1,0:T(8,128)(2,1)S(1)}, bf16[32,128]{1,0:T(8,128)(2,1)S(1)}, u32[]{:S(2)}, u32[]{:S(2)}) collective-permute-start(bf16[32,128]{1,0:T(8,128)(2,1)S(1)} %fusion.641), channel_id=1, source_target_pairs={{0,32},{32,64},{64,96},{96,128},{128,160},{160,192},{192,224},{224... | collective-permute-start | bytes 24584 | tf_op jit(solution)/shard_map/while/body/eval_jaxpr/ppermute | solution.py:12
  159.2 5.4 %collective-permute-start = (bf16[32,128]{1,0:T(8,128)(2,1)S(1)}, bf16[32,128]{1,0:T(8,128)(2,1)S(1)}, u32[]{:S(2)}, u32[]{:S(2)}) collective-permute-start(bf16[32,128]{1,0:T(8,128)(2,1)S(1)} %fusion.641), channel_id=1, source_target_pairs={{0,32},{32,64},{64,96},{96,128},{128,160},{160,192},{192,224},{224... | collective-permute-start | bytes 24584 | tf_op jit(solution)/shard_map/while/body/eval_jaxpr/ppermute | solution.py:12
  172.7 5.4 %collective-permute-start = (bf16[32,128]{1,0:T(8,128)(2,1)S(1)}, bf16[32,128]{1,0:T(8,128)(2,1)S(1)}, u32[]{:S(2)}, u32[]{:S(2)}) collective-permute-start(bf16[32,128]{1,0:T(8,128)(2,1)S(1)} %fusion.641), channel_id=1, source_target_pairs={{0,32},{32,64},{64,96},{96,128},{128,160},{160,192},{192,224},{224... | collective-permute-start | bytes 24584 | tf_op jit(solution)/shard_map/while/body/eval_jaxpr/ppermute | solution.py:12
  186.3 5.4 %collective-permute-start = (bf16[32,128]{1,0:T(8,128)(2,1)S(1)}, bf16[32,128]{1,0:T(8,128)(2,1)S(1)}, u32[]{:S(2)}, u32[]{:S(2)}) collective-permute-start(bf16[32,128]{1,0:T(8,128)(2,1)S(1)} %fusion.641), channel_id=1, source_target_pairs={{0,32},{32,64},{64,96},{96,128},{128,160},{160,192},{192,224},{224... | collective-permute-start | bytes 24584 | tf_op jit(solution)/shard_map/while/body/eval_jaxpr/ppermute | solution.py:12
  199.9 5.4 %collective-permute-start = (bf16[32,128]{1,0:T(8,128)(2,1)S(1)}, bf16[32,128]{1,0:T(8,128)(2,1)S(1)}, u32[]{:S(2)}, u32[]{:S(2)}) collective-permute-start(bf16[32,128]{1,0:T(8,128)(2,1)S(1)} %fusion.641), channel_id=1, source_target_pairs={{0,32},{32,64},{64,96},{96,128},{128,160},{160,192},{192,224},{224... | collective-permute-start | bytes 24584 | tf_op jit(solution)/shard_map/while/body/eval_jaxpr/ppermute | solution.py:12
  213.5 152.5 %while.21 = (s32[]{:T(128)}, bf16[32,128]{1,0:T(8,128)(2,1)S(1)}, s32[8,3]{1,0:T(8,128)S(1)}, bf16[8,3,128,128]{3,2,1,0:T(8,128)(2,1)S(1)}, bf16[8,128,128]{2,1,...) while((s32[]{:T(128)}, bf16[32,128]{1,0:T(8,128)(2,1)S(1)}, ...), condition=%wide.region_3.0_spmd, body=%wide.region_2.0_spmd.sunk | while | flops 34623628 | bytes 2516121 | solution.py:136
  219.4 4.8 %collective-permute-done.1 = bf16[32,128]{1,0:T(8,128)(2,1)S(1)} collective-permute-done((bf16[32,128]{1,0:T(8,128)(2,1)S(1)}, bf16[32,128]{1,0:T(8,128)(2,1)S(1)}, u32[]{:S(2)}, u32[]{:S(2)}) %collective-permute-start.1) | collective-permute-done | bytes 8224 | tf_op jit(solution)/shard_map/while/body/eval_jaxpr/ppermute | solution.py:12
  230.1 4.2 %collective-permute-done.1 = bf16[32,128]{1,0:T(8,128)(2,1)S(1)} collective-permute-done((bf16[32,128]{1,0:T(8,128)(2,1)S(1)}, bf16[32,128]{1,0:T(8,128)(2,1)S(1)}, u32[]{:S(2)}, u32[]{:S(2)}) %collective-permute-start.1) | collective-permute-done | bytes 8224 | tf_op jit(solution)/shard_map/while/body/eval_jaxpr/ppermute | solution.py:12
  240.2 4.2 %collective-permute-done.1 = bf16[32,128]{1,0:T(8,128)(2,1)S(1)} collective-permute-done((bf16[32,128]{1,0:T(8,128)(2,1)S(1)}, bf16[32,128]{1,0:T(8,128)(2,1)S(1)}, u32[]{:S(2)}, u32[]{:S(2)}) %collective-permute-start.1) | collective-permute-done | bytes 8224 | tf_op jit(solution)/shard_map/while/body/eval_jaxpr/ppermute | solution.py:12
  250.4 4.2 %collective-permute-done.1 = bf16[32,128]{1,0:T(8,128)(2,1)S(1)} collective-permute-done((bf16[32,128]{1,0:T(8,128)(2,1)S(1)}, bf16[32,128]{1,0:T(8,128)(2,1)S(1)}, u32[]{:S(2)}, u32[]{:S(2)}) %collective-permute-start.1) | collective-permute-done | bytes 8224 | tf_op jit(solution)/shard_map/while/body/eval_jaxpr/ppermute | solution.py:12
  260.5 4.2 %collective-permute-done.1 = bf16[32,128]{1,0:T(8,128)(2,1)S(1)} collective-permute-done((bf16[32,128]{1,0:T(8,128)(2,1)S(1)}, bf16[32,128]{1,0:T(8,128)(2,1)S(1)}, u32[]{:S(2)}, u32[]{:S(2)}) %collective-permute-start.1) | collective-permute-done | bytes 8224 | tf_op jit(solution)/shard_map/while/body/eval_jaxpr/ppermute | solution.py:12
  375.3 5.5 %collective-permute-start.5 = (bf16[4,32,128]{2,1,0:T(8,128)(2,1)S(1)}, bf16[4,32,128]{2,1,0:T(8,128)(2,1)S(1)}, u32[]{:S(2)}, u32[]{:S(2)}) collective-permute-start(bf16[4,32,128]{2,1,0:T(8,128)(2,1)S(1)} %get-tuple-element.255), channel_id=1, source_target_pairs={{1,0},{2,1},{3,2},{4,3},{5,4},{6,5},{7,6},{8,7},{9,8},{10,9},{11,1... | collective-permute-start | bytes 98312 | tf_op jit(solution)/shard_map/ppermute | solution.py:23
  380.8 5.4 %collective-permute-start.2 = (bf16[1,32,128]{2,1,0:T(8,128)(2,1)S(1)}, bf16[1,32,128]{2,1,0:T(8,128)(2,1)S(1)}, u32[]{:S(2)}, u32[]{:S(2)}) collective-permute-start(bf16[1,32,128]{2,1,0:T(8,128)(2,1)S(1)} %get-tuple-element.252), channel_id=1, source_target_pairs={{0,32},{32,64},{64,96},{96,128},{128,160},{160,192},{192,224},{224... | collective-permute-start | bytes 24584 | tf_op jit(solution)/shard_map/ppermute | solution.py:20
  (1342 shorter events, 272.6 us)
Async XLA Ops:
  23.4 6.2 %collective-permute-start = (bf16[32,128]{1,0:T(8,128)(2,1)S(1)}, bf16[32,128]{1,0:T(8,128)(2,1)S(1)}, u32[]{:S(2)}, u32[]{:S(2)}) collective-permute-start(bf16[32,128]{1,0:T(8,128)(2,1)S(1)} %fusion.641), channel_id=1, source_target_pairs={{0,32},{32,64},{64,96},{96,128},{128,160},{160,192},{192,224},{224... | collective-permute-start | bytes 24584 | tf_op jit(solution)/shard_map/while/body/eval_jaxpr/ppermute | solution.py:12
  37.0 6.2 %collective-permute-start = (bf16[32,128]{1,0:T(8,128)(2,1)S(1)}, bf16[32,128]{1,0:T(8,128)(2,1)S(1)}, u32[]{:S(2)}, u32[]{:S(2)}) collective-permute-start(bf16[32,128]{1,0:T(8,128)(2,1)S(1)} %fusion.641), channel_id=1, source_target_pairs={{0,32},{32,64},{64,96},{96,128},{128,160},{160,192},{192,224},{224... | collective-permute-start | bytes 24584 | tf_op jit(solution)/shard_map/while/body/eval_jaxpr/ppermute | solution.py:12
  50.6 6.2 %collective-permute-start = (bf16[32,128]{1,0:T(8,128)(2,1)S(1)}, bf16[32,128]{1,0:T(8,128)(2,1)S(1)}, u32[]{:S(2)}, u32[]{:S(2)}) collective-permute-start(bf16[32,128]{1,0:T(8,128)(2,1)S(1)} %fusion.641), channel_id=1, source_target_pairs={{0,32},{32,64},{64,96},{96,128},{128,160},{160,192},{192,224},{224... | collective-permute-start | bytes 24584 | tf_op jit(solution)/shard_map/while/body/eval_jaxpr/ppermute | solution.py:12
  64.1 6.2 %collective-permute-start = (bf16[32,128]{1,0:T(8,128)(2,1)S(1)}, bf16[32,128]{1,0:T(8,128)(2,1)S(1)}, u32[]{:S(2)}, u32[]{:S(2)}) collective-permute-start(bf16[32,128]{1,0:T(8,128)(2,1)S(1)} %fusion.641), channel_id=1, source_target_pairs={{0,32},{32,64},{64,96},{96,128},{128,160},{160,192},{192,224},{224... | collective-permute-start | bytes 24584 | tf_op jit(solution)/shard_map/while/body/eval_jaxpr/ppermute | solution.py:12
  77.7 6.2 %collective-permute-start = (bf16[32,128]{1,0:T(8,128)(2,1)S(1)}, bf16[32,128]{1,0:T(8,128)(2,1)S(1)}, u32[]{:S(2)}, u32[]{:S(2)}) collective-permute-start(bf16[32,128]{1,0:T(8,128)(2,1)S(1)} %fusion.641), channel_id=1, source_target_pairs={{0,32},{32,64},{64,96},{96,128},{128,160},{160,192},{192,224},{224... | collective-permute-start | bytes 24584 | tf_op jit(solution)/shard_map/while/body/eval_jaxpr/ppermute | solution.py:12
  91.3 6.2 %collective-permute-start = (bf16[32,128]{1,0:T(8,128)(2,1)S(1)}, bf16[32,128]{1,0:T(8,128)(2,1)S(1)}, u32[]{:S(2)}, u32[]{:S(2)}) collective-permute-start(bf16[32,128]{1,0:T(8,128)(2,1)S(1)} %fusion.641), channel_id=1, source_target_pairs={{0,32},{32,64},{64,96},{96,128},{128,160},{160,192},{192,224},{224... | collective-permute-start | bytes 24584 | tf_op jit(solution)/shard_map/while/body/eval_jaxpr/ppermute | solution.py:12
  104.9 6.2 %collective-permute-start = (bf16[32,128]{1,0:T(8,128)(2,1)S(1)}, bf16[32,128]{1,0:T(8,128)(2,1)S(1)}, u32[]{:S(2)}, u32[]{:S(2)}) collective-permute-start(bf16[32,128]{1,0:T(8,128)(2,1)S(1)} %fusion.641), channel_id=1, source_target_pairs={{0,32},{32,64},{64,96},{96,128},{128,160},{160,192},{192,224},{224... | collective-permute-start | bytes 24584 | tf_op jit(solution)/shard_map/while/body/eval_jaxpr/ppermute | solution.py:12
  118.4 6.2 %collective-permute-start = (bf16[32,128]{1,0:T(8,128)(2,1)S(1)}, bf16[32,128]{1,0:T(8,128)(2,1)S(1)}, u32[]{:S(2)}, u32[]{:S(2)}) collective-permute-start(bf16[32,128]{1,0:T(8,128)(2,1)S(1)} %fusion.641), channel_id=1, source_target_pairs={{0,32},{32,64},{64,96},{96,128},{128,160},{160,192},{192,224},{224... | collective-permute-start | bytes 24584 | tf_op jit(solution)/shard_map/while/body/eval_jaxpr/ppermute | solution.py:12
  132.0 6.2 %collective-permute-start = (bf16[32,128]{1,0:T(8,128)(2,1)S(1)}, bf16[32,128]{1,0:T(8,128)(2,1)S(1)}, u32[]{:S(2)}, u32[]{:S(2)}) collective-permute-start(bf16[32,128]{1,0:T(8,128)(2,1)S(1)} %fusion.641), channel_id=1, source_target_pairs={{0,32},{32,64},{64,96},{96,128},{128,160},{160,192},{192,224},{224... | collective-permute-start | bytes 24584 | tf_op jit(solution)/shard_map/while/body/eval_jaxpr/ppermute | solution.py:12
  145.6 6.2 %collective-permute-start = (bf16[32,128]{1,0:T(8,128)(2,1)S(1)}, bf16[32,128]{1,0:T(8,128)(2,1)S(1)}, u32[]{:S(2)}, u32[]{:S(2)}) collective-permute-start(bf16[32,128]{1,0:T(8,128)(2,1)S(1)} %fusion.641), channel_id=1, source_target_pairs={{0,32},{32,64},{64,96},{96,128},{128,160},{160,192},{192,224},{224... | collective-permute-start | bytes 24584 | tf_op jit(solution)/shard_map/while/body/eval_jaxpr/ppermute | solution.py:12
  159.2 6.2 %collective-permute-start = (bf16[32,128]{1,0:T(8,128)(2,1)S(1)}, bf16[32,128]{1,0:T(8,128)(2,1)S(1)}, u32[]{:S(2)}, u32[]{:S(2)}) collective-permute-start(bf16[32,128]{1,0:T(8,128)(2,1)S(1)} %fusion.641), channel_id=1, source_target_pairs={{0,32},{32,64},{64,96},{96,128},{128,160},{160,192},{192,224},{224... | collective-permute-start | bytes 24584 | tf_op jit(solution)/shard_map/while/body/eval_jaxpr/ppermute | solution.py:12
  172.7 6.2 %collective-permute-start = (bf16[32,128]{1,0:T(8,128)(2,1)S(1)}, bf16[32,128]{1,0:T(8,128)(2,1)S(1)}, u32[]{:S(2)}, u32[]{:S(2)}) collective-permute-start(bf16[32,128]{1,0:T(8,128)(2,1)S(1)} %fusion.641), channel_id=1, source_target_pairs={{0,32},{32,64},{64,96},{96,128},{128,160},{160,192},{192,224},{224... | collective-permute-start | bytes 24584 | tf_op jit(solution)/shard_map/while/body/eval_jaxpr/ppermute | solution.py:12
  186.3 6.2 %collective-permute-start = (bf16[32,128]{1,0:T(8,128)(2,1)S(1)}, bf16[32,128]{1,0:T(8,128)(2,1)S(1)}, u32[]{:S(2)}, u32[]{:S(2)}) collective-permute-start(bf16[32,128]{1,0:T(8,128)(2,1)S(1)} %fusion.641), channel_id=1, source_target_pairs={{0,32},{32,64},{64,96},{96,128},{128,160},{160,192},{192,224},{224... | collective-permute-start | bytes 24584 | tf_op jit(solution)/shard_map/while/body/eval_jaxpr/ppermute | solution.py:12
  199.9 6.2 %collective-permute-start = (bf16[32,128]{1,0:T(8,128)(2,1)S(1)}, bf16[32,128]{1,0:T(8,128)(2,1)S(1)}, u32[]{:S(2)}, u32[]{:S(2)}) collective-permute-start(bf16[32,128]{1,0:T(8,128)(2,1)S(1)} %fusion.641), channel_id=1, source_target_pairs={{0,32},{32,64},{64,96},{96,128},{128,160},{160,192},{192,224},{224... | collective-permute-start | bytes 24584 | tf_op jit(solution)/shard_map/while/body/eval_jaxpr/ppermute | solution.py:12
  217.5 6.7 %collective-permute-start.1 = (bf16[32,128]{1,0:T(8,128)(2,1)S(1)}, bf16[32,128]{1,0:T(8,128)(2,1)S(1)}, u32[]{:S(2)}, u32[]{:S(2)}) collective-permute-start(bf16[32,128]{1,0:T(8,128)(2,1)S(1)} %convolution_subtract_fusion.17), channel_id=1, source_target_pairs={{32,0},{64,32},{96,64},{128,96},{160,128},{192,160},{224,192},{256... | collective-permute-start | bytes 24584 | tf_op jit(solution)/shard_map/while/body/eval_jaxpr/ppermute | solution.py:12
  228.2 6.2 %collective-permute-start.1 = (bf16[32,128]{1,0:T(8,128)(2,1)S(1)}, bf16[32,128]{1,0:T(8,128)(2,1)S(1)}, u32[]{:S(2)}, u32[]{:S(2)}) collective-permute-start(bf16[32,128]{1,0:T(8,128)(2,1)S(1)} %convolution_subtract_fusion.17), channel_id=1, source_target_pairs={{32,0},{64,32},{96,64},{128,96},{160,128},{192,160},{224,192},{256... | collective-permute-start | bytes 24584 | tf_op jit(solution)/shard_map/while/body/eval_jaxpr/ppermute | solution.py:12
  238.3 6.2 %collective-permute-start.1 = (bf16[32,128]{1,0:T(8,128)(2,1)S(1)}, bf16[32,128]{1,0:T(8,128)(2,1)S(1)}, u32[]{:S(2)}, u32[]{:S(2)}) collective-permute-start(bf16[32,128]{1,0:T(8,128)(2,1)S(1)} %convolution_subtract_fusion.17), channel_id=1, source_target_pairs={{32,0},{64,32},{96,64},{128,96},{160,128},{192,160},{224,192},{256... | collective-permute-start | bytes 24584 | tf_op jit(solution)/shard_map/while/body/eval_jaxpr/ppermute | solution.py:12
  248.4 6.2 %collective-permute-start.1 = (bf16[32,128]{1,0:T(8,128)(2,1)S(1)}, bf16[32,128]{1,0:T(8,128)(2,1)S(1)}, u32[]{:S(2)}, u32[]{:S(2)}) collective-permute-start(bf16[32,128]{1,0:T(8,128)(2,1)S(1)} %convolution_subtract_fusion.17), channel_id=1, source_target_pairs={{32,0},{64,32},{96,64},{128,96},{160,128},{192,160},{224,192},{256... | collective-permute-start | bytes 24584 | tf_op jit(solution)/shard_map/while/body/eval_jaxpr/ppermute | solution.py:12
  268.7 6.2 %collective-permute-start.1 = (bf16[32,128]{1,0:T(8,128)(2,1)S(1)}, bf16[32,128]{1,0:T(8,128)(2,1)S(1)}, u32[]{:S(2)}, u32[]{:S(2)}) collective-permute-start(bf16[32,128]{1,0:T(8,128)(2,1)S(1)} %convolution_subtract_fusion.17), channel_id=1, source_target_pairs={{32,0},{64,32},{96,64},{128,96},{160,128},{192,160},{224,192},{256... | collective-permute-start | bytes 24584 | tf_op jit(solution)/shard_map/while/body/eval_jaxpr/ppermute | solution.py:12
  278.8 6.2 %collective-permute-start.1 = (bf16[32,128]{1,0:T(8,128)(2,1)S(1)}, bf16[32,128]{1,0:T(8,128)(2,1)S(1)}, u32[]{:S(2)}, u32[]{:S(2)}) collective-permute-start(bf16[32,128]{1,0:T(8,128)(2,1)S(1)} %convolution_subtract_fusion.17), channel_id=1, source_target_pairs={{32,0},{64,32},{96,64},{128,96},{160,128},{192,160},{224,192},{256... | collective-permute-start | bytes 24584 | tf_op jit(solution)/shard_map/while/body/eval_jaxpr/ppermute | solution.py:12
  370.1 19.2 %collective-permute-start.3 = (bf16[1,32,128]{2,1,0:T(8,128)(2,1)S(1)}, bf16[1,32,128]{2,1,0:T(8,128)(2,1)S(1)}, u32[]{:S(2)}, u32[]{:S(2)}) collective-permute-start(bf16[1,32,128]{2,1,0:T(8,128)(2,1)S(1)} %get-tuple-element.253), channel_id=1, source_target_pairs={{32,0},{64,32},{96,64},{128,96},{160,128},{192,160},{224,192},{256... | collective-permute-start | bytes 24584 | tf_op jit(solution)/shard_map/ppermute | solution.py:23
  372.2 17.5 %collective-permute-start.4 = (bf16[4,32,128]{2,1,0:T(8,128)(2,1)S(1)}, bf16[4,32,128]{2,1,0:T(8,128)(2,1)S(1)}, u32[]{:S(2)}, u32[]{:S(2)}) collective-permute-start(bf16[4,32,128]{2,1,0:T(8,128)(2,1)S(1)} %get-tuple-element.254), channel_id=1, source_target_pairs={{0,1},{1,2},{2,3},{3,4},{4,5},{5,6},{6,7},{7,8},{8,9},{9,10},{10,1... | collective-permute-start | bytes 98312 | tf_op jit(solution)/shard_map/ppermute | solution.py:20
  375.3 14.3 %collective-permute-start.5 = (bf16[4,32,128]{2,1,0:T(8,128)(2,1)S(1)}, bf16[4,32,128]{2,1,0:T(8,128)(2,1)S(1)}, u32[]{:S(2)}, u32[]{:S(2)}) collective-permute-start(bf16[4,32,128]{2,1,0:T(8,128)(2,1)S(1)} %get-tuple-element.255), channel_id=1, source_target_pairs={{1,0},{2,1},{3,2},{4,3},{5,4},{6,5},{7,6},{8,7},{9,8},{10,9},{11,1... | collective-permute-start | bytes 98312 | tf_op jit(solution)/shard_map/ppermute | solution.py:23
  380.8 9.7 %collective-permute-start.2 = (bf16[1,32,128]{2,1,0:T(8,128)(2,1)S(1)}, bf16[1,32,128]{2,1,0:T(8,128)(2,1)S(1)}, u32[]{:S(2)}, u32[]{:S(2)}) collective-permute-start(bf16[1,32,128]{2,1,0:T(8,128)(2,1)S(1)} %get-tuple-element.252), channel_id=1, source_target_pairs={{0,32},{32,64},{64,96},{96,128},{128,160},{160,192},{192,224},{224... | collective-permute-start | bytes 24584 | tf_op jit(solution)/shard_map/ppermute | solution.py:20
  (65 other events, 593.2 us)
where the time goes:
time: 394 us; the launch traced here: 392 us
  matrix products  174 us (44%)
  starting transfers between devices  126 us (32%)
  waiting for transfers between devices  75.8 us (19%)
  local copies, waits for them, and re-layouts  8.74 us (2%)
  loops' own time  4.45 us (1%)
    ppermute x30, starting transfers between devices, shifted(): lax.ppermute(value, axis, [(source, source + steps) for source in range(f...  109 us
    dot_general x128, matrix products, solve_down(): result = jnp.dot(gap, inverse[position], preferred_element_type=jnp.float32)  91.2 us
    ppermute x30, waiting for transfers between devices, shifted(): lax.ppermute(value, axis, [(source, source + steps) for source in range(f...  75.8 us
    dot_general x224, matrix products, select_rows(): jnp.einsum('sr,rqb->sqb', weights, candidates, preferred_element_type=jnp...  47.6 us
    dot_general x128, matrix products, solve_up(): jnp.dot(summed.astype(jnp.bfloat16), inverse[position], preferred_element...  33.1 us
    ppermute x2, starting transfers between devices, extended(): lax.ppermute(lax.slice_in_dim(block, block.shape[dim] - width, None, axis...  8.53 us
  transfers between devices with their start and end apart: 34, of which 30 were waited for; matrix products, arithmetic and copies ran while one was open for 1% of the time, Pallas kernels for 0%

commit v1 on v0

v1 whole, which is shorter than its diff:
```python
import functools

import jax
import jax.numpy as jnp
from jax import lax
from jax.experimental import pallas as pl
from jax.experimental.pallas import tpu as pltpu
from jax.sharding import PartitionSpec as P

F32 = jnp.float32
BF16 = jnp.bfloat16
MESH = pl.DeviceIdType.MESH
ROWS = 8
BLK = 128
NRHS = 32
RIM = 4
AFFINE = BLK + NRHS
WIDE = AFFINE + BLK
ELEMENT = AFFINE + WIDE
PIECES = ((0, AFFINE), (AFFINE, 2 * AFFINE), (2 * AFFINE, ELEMENT))


def dot(left, right):
    return jnp.dot(left.astype(BF16), right, preferred_element_type=F32)


def joined(left, right):
    right_m, right_a = right[:BLK], right[BLK:AFFINE]
    right_h, right_b = right[AFFINE : AFFINE + BLK], right[AFFINE + BLK : 2 * AFFINE]
    right_k, left_k = right[2 * AFFINE :], left[2 * AFFINE :]
    through = dot(left[:AFFINE], jnp.concatenate([right_m, right_h], axis=1))
    onward = jnp.concatenate(
        [through[:BLK, :BLK], through[BLK:, :BLK] + right_a.astype(F32)], axis=0
    )
    back = jnp.concatenate(
        [
            through[:BLK, BLK:].astype(BF16),
            (through[BLK:, BLK:] + right_b.astype(F32)).astype(BF16),
            right_k,
        ],
        axis=0,
    )
    back = dot(back, left_k)
    back = jnp.concatenate(
        [back[:AFFINE] + left[AFFINE : 2 * AFFINE].astype(F32), back[AFFINE:]], axis=0
    )
    return onward.astype(BF16), back.astype(BF16)


def kernel(
    sections,
    parts,
    lower_index,
    upper_index,
    halo_index,
    rhs_hbm,
    inverse_hbm,
    diag_hbm,
    lower_hbm,
    upper_hbm,
    halo_hbm,
    solution_ref,
    product_ref,
    rhs,
    inverse,
    diag,
    lower,
    upper,
    halo,
    fwd,
    fwd_wide,
    bwd,
    bwd_values,
    pair,
    ring,
    ends,
    last_own,
    last_in,
    rows,
    rim,
    load_sem,
    pair_send,
    pair_recv,
    ring_send,
    ring_recv,
    ends_send,
    ends_recv,
    last_send,
    last_recv,
    rim_send,
    rim_recv,
):
    chips = sections // 2
    left_hops = chips // 2
    right_hops = chips - 1 - left_hops
    section = lax.axis_index("section")
    part = lax.axis_index("dom")
    core = lax.rem(section, 2)
    chip = lax.div(section, 2)
    sibling = (section + 1 - 2 * core, part)
    onto = (2 * lax.rem(chip + 1 - 2 * core + chips, chips) + core, part)
    other = (2 * lax.rem(chip + 2 * core - 1 + chips, chips) + core, part)
    following = (lax.rem(section + 1, sections), part)
    beyond = (lax.rem(section + 2 * core - 1 + sections, sections), part)
    part_up = (section, lax.rem(part + 1, parts))
    part_down = (section, lax.rem(part + parts - 1, parts))

    loads = []
    for place, (source, target) in enumerate(
        (
            (lower_hbm, lower),
            (inverse_hbm, inverse),
            (rhs_hbm, rhs),
            (upper_hbm, upper),
            (diag_hbm, diag),
            (halo_hbm, halo),
        )
    ):
        copy = pltpu.make_async_copy(source, target, load_sem.at[place])
        copy.start()
        loads.append(copy)

    barrier = pltpu.get_barrier_semaphore()
    for device in (sibling, onto, other, beyond, part_up, part_down):
        pl.semaphore_signal(barrier, inc=1, device_id=device, device_id_type=MESH)

    spread = lax.broadcasted_iota(jnp.int32, (BLK, BLK), 0)
    identity = (spread == lax.broadcasted_iota(jnp.int32, (BLK, BLK), 1)).astype(F32)
    has_before = (section > 0).astype(F32)
    has_after = (section < sections - 1).astype(F32)
    fwd[ROWS, :BLK] = (identity * has_before).astype(BF16)
    fwd[ROWS, BLK:] = jnp.zeros((NRHS, BLK), BF16)
    bwd[ROWS, :AFFINE] = jnp.zeros((AFFINE, BLK), BF16)
    bwd[ROWS, AFFINE:] = (identity * has_after).astype(BF16)

    for copy in loads[:3]:
        copy.wait()
    for k in range(ROWS):
        folded = dot(lower[k].reshape(3 * BLK, BLK), inverse[k])
        base = jnp.concatenate([folded[:BLK] * -has_before, dot(rhs[k], inverse[k])], axis=0)
        slots = [jnp.where(lower_index[k, m] == k, ROWS, lower_index[k, m]) for m in (1, 2)]
        sources = jnp.concatenate([fwd[slot] for slot in slots], axis=1)
        wide = base - dot(sources, folded[BLK:].astype(BF16))
        fwd_wide[k] = wide
        fwd[k] = wide.astype(BF16)
    pair[core, :AFFINE] = fwd[ROWS - 1]

    pl.semaphore_wait(barrier, 6)

    def pair_copy(piece, low, high):
        return pltpu.make_async_remote_copy(
            src_ref=pair.at[core, pl.ds(low, high - low)],
            dst_ref=pair.at[core, pl.ds(low, high - low)],
            send_sem=pair_send.at[piece],
            recv_sem=pair_recv.at[piece],
            device_id=sibling,
            device_id_type=MESH,
        )

    pair_onward = pair_copy(0, 0, AFFINE)
    pair_back = pair_copy(1, AFFINE, ELEMENT)
    pair_onward.start()

    loads[3].wait()
    for k in range(ROWS - 1, -1, -1):
        folded = dot(upper[k].reshape(3 * BLK, BLK), inverse[k])
        if k == ROWS - 1:
            last_own[...] = (folded[:BLK] + folded[BLK : 2 * BLK] + folded[2 * BLK :]).astype(BF16)
            last_copy = pltpu.make_async_remote_copy(
                src_ref=last_own,
                dst_ref=last_in,
                send_sem=last_send.at[0],
                recv_sem=last_recv.at[0],
                device_id=following,
                device_id_type=MESH,
            )
            last_copy.start()
        base = jnp.concatenate([fwd_wide[k], folded[:BLK] * -has_after], axis=0)
        slots = [jnp.where(upper_index[k, m] == k, ROWS, upper_index[k, m]) for m in (1, 2)]
        sources = jnp.concatenate([bwd[slot] for slot in slots], axis=1)
        wide = base - dot(sources, folded[BLK:].astype(BF16))
        bwd_values[k] = wide[BLK:AFFINE]
        bwd[k] = wide.astype(BF16)
    pair[core, AFFINE:] = bwd[0]
    pair_back.start()
    pair_onward.wait_recv()
    pair_back.wait_recv()
    onward, back = joined(pair[0], pair[1])
    ring[0, :AFFINE] = onward
    ring[0, AFFINE:] = back

    def ring_copy(hop, piece):
        low, high = PIECES[piece]
        return pltpu.make_async_remote_copy(
            src_ref=ring.at[hop, pl.ds(low, high - low)],
            dst_ref=ring.at[hop + 1, pl.ds(low, high - low)],
            send_sem=ring_send.at[hop, piece],
            recv_sem=ring_recv.at[hop, piece],
            device_id=onto,
            device_id_type=MESH,
        )

    for piece in range(len(PIECES)):
        ring_copy(0, piece).start()

    def take(hop, last):
        for piece in range(len(PIECES)):
            ring_copy(hop - 1, piece).wait_recv()
            if not last:
                ring_copy(hop, piece).start()

    def fold(hop, target, place):
        done = 1 if hop == 2 else left_hops + 1
        left = ring[jnp.where(core == 0, hop, done)]
        right = ring[jnp.where(core == 0, done, hop)]
        onward, back = joined(left, right)
        target[place, :AFFINE] = onward
        target[place, AFFINE:] = back

    for hop in range(1, right_hops):
        take(hop, False)
        if hop >= 2:
            fold(hop, ring, left_hops + 1)

    @pl.when(core == 0)
    def _():
        for hop in range(right_hops, left_hops + 1):
            take(hop, hop == left_hops)
            if hop == left_hops:
                fold(hop, ends, 0)
            elif hop >= 2:
                fold(hop, ring, left_hops + 1)

    @pl.when(core == 1)
    def _():
        take(right_hops, True)
        if right_hops >= 2:
            fold(right_hops, ends, 1)
        else:
            ends[1] = ring[1]

    ends_copy = pltpu.make_async_remote_copy(
        src_ref=ends.at[core],
        dst_ref=ends.at[core],
        send_sem=ends_send.at[0],
        recv_sem=ends_recv.at[0],
        device_id=sibling,
        device_id_type=MESH,
    )
    ends_copy.start()
    ends_copy.wait_recv()

    def value(ref, place, low, size):
        return ref[place, low : low + size]

    inflow = value(ends, 0, BLK, NRHS).astype(F32) + dot(
        value(ends, 1, BLK, NRHS), value(ends, 0, 0, BLK)
    )
    middle = value(pair, 0, BLK, NRHS).astype(F32) + dot(inflow, value(pair, 0, 0, BLK))
    outgoing = value(pair, 1, BLK, NRHS).astype(F32) + dot(middle, value(pair, 1, 0, BLK))
    far = value(ends, 1, BLK, NRHS).astype(F32) + dot(outgoing, value(ends, 1, 0, BLK))
    near = dot(outgoing, value(ends, 1, AFFINE, BLK))
    far = value(ends, 0, AFFINE + BLK, NRHS).astype(F32) + dot(far, value(ends, 0, AFFINE, BLK))
    outflow = (
        value(ends, 1, AFFINE + BLK, NRHS).astype(F32)
        + near
        + dot(far, value(ends, 1, 2 * AFFINE, BLK))
    )
    centre = (
        value(pair, 1, AFFINE + BLK, NRHS).astype(F32)
        + dot(middle, value(pair, 1, AFFINE, BLK))
        + dot(outflow, value(pair, 1, 2 * AFFINE, BLK))
    )
    inflow = jnp.where(core == 0, inflow, middle)
    outflow = jnp.where(core == 0, centre, outflow)
    flows = jnp.concatenate([inflow, outflow], axis=1).astype(BF16)
    for k in range(ROWS):
        response = jnp.concatenate([bwd[k, :BLK], bwd[k, AFFINE:]], axis=0)
        solved = bwd_values[k] + dot(flows, response)
        solution_ref[k] = solved
        rows[k] = solved.astype(BF16)

    rim_copies = [
        pltpu.make_async_remote_copy(
            src_ref=rows.at[pl.ds(ROWS - RIM, RIM)],
            dst_ref=rim.at[pl.ds(0, RIM)],
            send_sem=rim_send.at[0],
            recv_sem=rim_recv.at[0],
            device_id=part_up,
            device_id_type=MESH,
        ),
        pltpu.make_async_remote_copy(
            src_ref=rows.at[pl.ds(0, RIM)],
            dst_ref=rim.at[pl.ds(RIM, RIM)],
            send_sem=rim_send.at[1],
            recv_sem=rim_recv.at[1],
            device_id=part_down,
            device_id_type=MESH,
        ),
    ]
    for copy in rim_copies:
        copy.start()

    last_copy.wait_recv()
    edges_before = (inflow - dot(rows[0], last_in[...])) * has_before
    edges = pair_edges = jnp.stack([edges_before, outflow * has_after]).astype(BF16)
    rows[pl.ds(ROWS, 2)] = edges
    for copy in loads[4:]:
        copy.wait()
    totals = []
    for k in range(ROWS):
        lows = [rows[jnp.where(lower_index[k, m] == k, ROWS, lower_index[k, m])] for m in range(3)]
        highs = [
            rows[jnp.where(upper_index[k, m] == k, ROWS + 1, upper_index[k, m])] for m in range(3)
        ]
        total = dot(rows[k], diag[k])
        total = total + dot(jnp.concatenate(lows, axis=1), lower[k].reshape(3 * BLK, BLK))
        total = total + dot(jnp.concatenate(highs, axis=1), upper[k].reshape(3 * BLK, BLK))
        product_ref[k] = total

    for copy in rim_copies:
        copy.wait_recv()

    @pl.when(part == 0)
    def _():
        rim[pl.ds(0, RIM)] = jnp.zeros((RIM, NRHS, BLK), BF16)

    @pl.when(part == parts - 1)
    def _():
        rim[pl.ds(RIM, RIM)] = jnp.zeros((RIM, NRHS, BLK), BF16)

    for k in range(ROWS):
        sources = jnp.concatenate([rim[halo_index[k, h]] for h in range(2)], axis=1)
        product_ref[k] = product_ref[k] + dot(sources, halo[k].reshape(2 * BLK, BLK))

    pair_onward.wait_send()
    pair_back.wait_send()
    last_copy.wait_send()
    ends_copy.wait_send()
    for copy in rim_copies:
        copy.wait_send()
    for hop in range(right_hops):
        for piece in range(len(PIECES)):
            ring_copy(hop, piece).wait_send()

    @pl.when(core == 0)
    def _():
        for hop in range(right_hops, left_hops):
            for piece in range(len(PIECES)):
                ring_copy(hop, piece).wait_send()


def on_device(sections, parts, rhs, inverse, diag, lower, upper, halo, low_index, up_index, halo_index):
    chips = sections // 2
    hops = chips // 2
    smem = pl.BlockSpec(memory_space=pltpu.SMEM)
    hbm = pl.BlockSpec(memory_space=pl.ANY)
    vmem = pl.BlockSpec(memory_space=pltpu.VMEM)
    dma = pltpu.SemaphoreType.DMA
    return pl.pallas_call(
        functools.partial(kernel, sections, parts),
        out_shape=(
            jax.ShapeDtypeStruct(rhs.shape, F32),
            jax.ShapeDtypeStruct(rhs.shape, F32),
        ),
        in_specs=[smem] * 3 + [hbm] * 6,
        out_specs=(vmem, vmem),
        scratch_shapes=[
            pltpu.VMEM(rhs.shape, F32),
            pltpu.VMEM(inverse.shape, BF16),
            pltpu.VMEM(diag.shape, BF16),
            pltpu.VMEM(lower.shape, BF16),
            pltpu.VMEM(upper.shape, BF16),
            pltpu.VMEM(halo.shape, BF16),
            pltpu.VMEM((ROWS + 1, AFFINE, BLK), BF16),
            pltpu.VMEM((ROWS, AFFINE, BLK), F32),
            pltpu.VMEM((ROWS + 1, WIDE, BLK), BF16),
            pltpu.VMEM((ROWS, NRHS, BLK), F32),
            pltpu.VMEM((2, ELEMENT, BLK), BF16),
            pltpu.VMEM((hops + 2, ELEMENT, BLK), BF16),
            pltpu.VMEM((2, ELEMENT, BLK), BF16),
            pltpu.VMEM((BLK, BLK), BF16),
            pltpu.VMEM((BLK, BLK), BF16),
            pltpu.VMEM((ROWS + 2, NRHS, BLK), BF16),
            pltpu.VMEM((2 * RIM, NRHS, BLK), BF16),
            dma((6,)),
            dma((2,)),
            dma((2,)),
            dma((hops, len(PIECES))),
            dma((hops, len(PIECES))),
            dma((1,)),
            dma((1,)),
            dma((1,)),
            dma((1,)),
            dma((2,)),
            dma((2,)),
        ],
        compiler_params=pltpu.CompilerParams(collective_id=0, has_side_effects=True),
        name="block_ilu_apply",
    )(low_index, up_index, halo_index, rhs, inverse, diag, lower, upper, halo)


def solution(mesh):
    row = ("section", "dom")
    in_specs = (
        P(row, None, None),
        P(row, None, None),
        P(row, None, None),
        P(row, None, None, None),
        P(row, None, None, None),
        P(row, None, None, None),
        P(row, None),
        P(row, None),
        P(row, None),
    )
    out_specs = (P(row, None, None), P(row, None, None))
    body = functools.partial(on_device, mesh.shape["section"], mesh.shape["dom"])
    return jax.shard_map(
        body, mesh=mesh, in_specs=in_specs, out_specs=out_specs, check_vma=False
    )
```

time: 394 us -> 46.2 us (0.12)
  the two profiles are of different devices: /device:TPU:281 before, /device:TPU:1 now
where the time goes in v1:
time: 46.2 us; the launch traced here: 46 us
  Pallas kernels  40.4 us (87%)
  local copies, waits for them, and re-layouts  4.97 us (11%)
  between operations  0.66 us (1%)
    pallas_call x1, Pallas kernels, on_device(): pl.pallas_call(functools.partial(kernel, sections, parts), out_shape=(jax...  40.4 us
    unnamed x11, local copies, waits for them, and re-layouts  4.97 us

profile of v1, /device:TPU:1, one launch (start us, length us, event | category | flops | bytes accessed | tf_op | source)
XLA Modules:
  0.0 46.0 jit_solution(8626771953977598650)
XLA Ops:
  0.6 0.0 copy-start.1
  0.6 1.4 %copy.11.lower_index = s32[8,3]{1,0:T(8,128)} copy(s32[8,3]{0,1:T(4,128)} %param.15) | data formatting | bytes 192 | tf_op args[6]
  2.0 0.0 copy-done.1
  2.0 0.0 copy-start.2
  2.0 0.7 %copy.12.upper_index = s32[8,3]{1,0:T(8,128)} copy(s32[8,3]{0,1:T(4,128)S(1)} %copy-done.1) | data formatting | bytes 192 | tf_op args[7]
  2.7 0.0 copy-done.2
  2.7 0.7 %copy.13.halo_index = s32[8,2]{1,0:T(8,128)} copy(s32[8,2]{0,1:T(2,128)S(1)} %copy-done.2) | data formatting | bytes 128 | tf_op args[8]
  3.3 40.4 %block_ilu_apply.1 = (f32[8,32,128]{2,1,0:T(8,128)}, f32[8,32,128]{2,1,0:T(8,128)}) custom-call(s32[8,3]{1,0:T(8,128)} %copy.11.lower_index, s32[8,3]{1,0:T(8,128)} %copy.12.upper_index, s32[8,2]{1,0:T(8,128)} %copy.13.halo_index, f32[8,32,128]{2,1,0:T(8,128)} %rhs_hbm.1, bf16[8,128,128]{2,1,0:T(8,128)(2,1)} %inverse_hbm.1, bf16[8,128,128]{2,1,0:T(8,128)(2,1)} %diag_hbm.1, ...), custom_call_target="tpu_custom_call" | custom-call | tf_op jit(solution)/shard_map/block_ilu_apply/pallas_call | solution.py:360
  43.7 0.0 copy-start
  43.7 1.6 %copy.16 = f32[8,32,128]{2,1,0:T(8,128)} copy(f32[8,32,128]{2,1,0:T(8,128)} %get-tuple-element.4) | data formatting | bytes 262144
  45.3 0.0 copy-done
  45.3 0.7 %copy.17 = f32[8,32,128]{2,1,0:T(8,128)} copy(f32[8,32,128]{2,1,0:T(8,128)S(1)} %copy-done) | data formatting | bytes 262144
Async XLA Ops:
  0.6 1.4 %copy-start.1 = (s32[8,3]{0,1:T(4,128)S(1)}, s32[8,3]{0,1:T(4,128)}, u32[]{:S(2)}) copy-start(s32[8,3]{0,1:T(4,128)} %param.16) | copy-start | bytes 292
  2.0 0.7 %copy-start.2 = (s32[8,2]{0,1:T(2,128)S(1)}, s32[8,2]{0,1:T(2,128)}, u32[]{:S(2)}) copy-start(s32[8,2]{0,1:T(2,128)} %param.17) | copy-start | bytes 196
  43.7 1.6 %copy-start = (f32[8,32,128]{2,1,0:T(8,128)S(1)}, f32[8,32,128]{2,1,0:T(8,128)}, u32[]{:S(2)}) copy-start(f32[8,32,128]{2,1,0:T(8,128)} %get-tuple-element.5) | copy-start | bytes 393220

commit v2 on v1

--- a/solution.py
+++ b/solution.py
@@ -102,8 +102,8 @@
     other = (2 * lax.rem(chip + 2 * core - 1 + chips, chips) + core, part)
     following = (lax.rem(section + 1, sections), part)
     beyond = (lax.rem(section + 2 * core - 1 + sections, sections), part)
-    part_up = (section, lax.rem(part + 1, parts))
-    part_down = (section, lax.rem(part + parts - 1, parts))
+    part_up = (section, lax.min(part + 1, parts - 1))
+    part_down = (section, lax.max(part - 1, 0))
 
     loads = []
     for place, (source, target) in enumerate(
@@ -121,8 +121,24 @@
         loads.append(copy)
 
     barrier = pltpu.get_barrier_semaphore()
-    for device in (sibling, onto, other, beyond, part_up, part_down):
+    for device in (sibling, onto, other, beyond):
         pl.semaphore_signal(barrier, inc=1, device_id=device, device_id_type=MESH)
+
+    @pl.when(part < parts - 1)
+    def _():
+        pl.semaphore_signal(barrier, inc=1, device_id=part_up, device_id_type=MESH)
+
+    @pl.when(part > 0)
+    def _():
+        pl.semaphore_signal(barrier, inc=1, device_id=part_down, device_id_type=MESH)
+
+    @pl.when(part == 0)
+    def _():
+        rim[pl.ds(0, RIM)] = jnp.zeros((RIM, NRHS, BLK), BF16)
+
+    @pl.when(part == parts - 1)
+    def _():
+        rim[pl.ds(RIM, RIM)] = jnp.zeros((RIM, NRHS, BLK), BF16)
 
     spread = lax.broadcasted_iota(jnp.int32, (BLK, BLK), 0)
     identity = (spread == lax.broadcasted_iota(jnp.int32, (BLK, BLK), 1)).astype(F32)
@@ -138,14 +154,15 @@
     for k in range(ROWS):
         folded = dot(lower[k].reshape(3 * BLK, BLK), inverse[k])
         base = jnp.concatenate([folded[:BLK] * -has_before, dot(rhs[k], inverse[k])], axis=0)
-        slots = [jnp.where(lower_index[k, m] == k, ROWS, lower_index[k, m]) for m in (1, 2)]
+        slots = [jnp.where(lower_index[m, k] == k, ROWS, lower_index[m, k]) for m in (1, 2)]
         sources = jnp.concatenate([fwd[slot] for slot in slots], axis=1)
         wide = base - dot(sources, folded[BLK:].astype(BF16))
         fwd_wide[k] = wide
         fwd[k] = wide.astype(BF16)
     pair[core, :AFFINE] = fwd[ROWS - 1]
 
-    pl.semaphore_wait(barrier, 6)
+    partners = 4 + (part < parts - 1).astype(jnp.int32) + (part > 0).astype(jnp.int32)
+    pl.semaphore_wait(barrier, partners)
 
     def pair_copy(piece, low, high):
         return pltpu.make_async_remote_copy(
@@ -176,7 +193,7 @@
             )
             last_copy.start()
         base = jnp.concatenate([fwd_wide[k], folded[:BLK] * -has_after], axis=0)
-        slots = [jnp.where(upper_index[k, m] == k, ROWS, upper_index[k, m]) for m in (1, 2)]
+        slots = [jnp.where(upper_index[m, k] == k, ROWS, upper_index[m, k]) for m in (1, 2)]
         sources = jnp.concatenate([bwd[slot] for slot in slots], axis=1)
         wide = base - dot(sources, folded[BLK:].astype(BF16))
         bwd_values[k] = wide[BLK:AFFINE]
@@ -298,47 +315,56 @@
             device_id_type=MESH,
         ),
     ]
-    for copy in rim_copies:
-        copy.start()
+    @pl.when(part < parts - 1)
+    def _():
+        rim_copies[0].start()
+
+    @pl.when(part > 0)
+    def _():
+        rim_copies[1].start()
 
     last_copy.wait_recv()
     edges_before = (inflow - dot(rows[0], last_in[...])) * has_before
-    edges = pair_edges = jnp.stack([edges_before, outflow * has_after]).astype(BF16)
+    edges = jnp.stack([edges_before, outflow * has_after]).astype(BF16)
     rows[pl.ds(ROWS, 2)] = edges
     for copy in loads[4:]:
         copy.wait()
     totals = []
     for k in range(ROWS):
-        lows = [rows[jnp.where(lower_index[k, m] == k, ROWS, lower_index[k, m])] for m in range(3)]
+        lows = [rows[jnp.where(lower_index[m, k] == k, ROWS, lower_index[m, k])] for m in range(3)]
         highs = [
-            rows[jnp.where(upper_index[k, m] == k, ROWS + 1, upper_index[k, m])] for m in range(3)
+            rows[jnp.where(upper_index[m, k] == k, ROWS + 1, upper_index[m, k])] for m in range(3)
         ]
         total = dot(rows[k], diag[k])
         total = total + dot(jnp.concatenate(lows, axis=1), lower[k].reshape(3 * BLK, BLK))
         total = total + dot(jnp.concatenate(highs, axis=1), upper[k].reshape(3 * BLK, BLK))
         product_ref[k] = total
 
-    for copy in rim_copies:
-        copy.wait_recv()
-
-    @pl.when(part == 0)
-    def _():
-        rim[pl.ds(0, RIM)] = jnp.zeros((RIM, NRHS, BLK), BF16)
-
-    @pl.when(part == parts - 1)
-    def _():
-        rim[pl.ds(RIM, RIM)] = jnp.zeros((RIM, NRHS, BLK), BF16)
+    @pl.when(part > 0)
+    def _():
+        rim_copies[0].wait_recv()
+
+    @pl.when(part < parts - 1)
+    def _():
+        rim_copies[1].wait_recv()
 
     for k in range(ROWS):
-        sources = jnp.concatenate([rim[halo_index[k, h]] for h in range(2)], axis=1)
+        sources = jnp.concatenate([rim[halo_index[h, k]] for h in range(2)], axis=1)
         product_ref[k] = product_ref[k] + dot(sources, halo[k].reshape(2 * BLK, BLK))
 
     pair_onward.wait_send()
     pair_back.wait_send()
     last_copy.wait_send()
     ends_copy.wait_send()
-    for copy in rim_copies:
-        copy.wait_send()
+
+    @pl.when(part < parts - 1)
+    def _():
+        rim_copies[0].wait_send()
+
+    @pl.when(part > 0)
+    def _():
+        rim_copies[1].wait_send()
+
     for hop in range(right_hops):
         for piece in range(len(PIECES)):
             ring_copy(hop, piece).wait_send()
@@ -360,8 +386,8 @@
     return pl.pallas_call(
         functools.partial(kernel, sections, parts),
         out_shape=(
-            jax.ShapeDtypeStruct(rhs.shape, F32),
-            jax.ShapeDtypeStruct(rhs.shape, F32),
+            pltpu.VMEM(rhs.shape, F32),
+            pltpu.VMEM(rhs.shape, F32),
         ),
         in_specs=[smem] * 3 + [hbm] * 6,
         out_specs=(vmem, vmem),
@@ -397,7 +423,7 @@
         ],
         compiler_params=pltpu.CompilerParams(collective_id=0, has_side_effects=True),
         name="block_ilu_apply",
-    )(low_index, up_index, halo_index, rhs, inverse, diag, lower, upper, halo)
+    )(low_index.T, up_index.T, halo_index.T, rhs, inverse, diag, lower, upper, halo)
 
 
 def solution(mesh):

time: 46.2 us -> 33.1 us (0.72)
  the two profiles are of different devices: /device:TPU:1 before, /device:TPU:199 now
where the time goes in v2:
time: 33.1 us; the launch traced here: 33 us
  Pallas kernels  31 us (94%)
  local copies, waits for them, and re-layouts  1.31 us (4%)
  between operations  0.64 us (2%)
    pallas_call x1, Pallas kernels, on_device(): pl.pallas_call(functools.partial(kernel, sections, parts), out_shape=(plt...  31 us
    unnamed x2, local copies, waits for them, and re-layouts  1.31 us

profile of v2, /device:TPU:199, one launch (start us, length us, event | category | flops | bytes accessed | tf_op | source)
XLA Modules:
  0.0 33.0 jit_solution(8786225028382057983)
XLA Ops:
  0.6 31.0 %block_ilu_apply.1 = (f32[8,32,128]{2,1,0:T(8,128)S(1)}, f32[8,32,128]{2,1,0:T(8,128)S(1)}) custom-call(s32[3,8]{1,0:T(4,128)} %bitcast.3, s32[3,8]{1,0:T(4,128)} %bitcast.4, s32[2,8]{1,0:T(2,128)} %bitcast.5, f32[8,32,128]{2,1,0:T(8,128)} %rhs_hbm.1, bf16[8,128,128]{2,1,0:T(8,128)(2,1)} %inverse_hbm.1, bf16[8,128,128]{2,1,0:T(8,128)(2,1)} %diag_hbm.1, ...), custom_call_target="tpu_custom_call" | custom-call | tf_op jit(solution)/shard_map/block_ilu_apply/pallas_call | solution.py:386
  31.7 0.7 %copy.13 = f32[8,32,128]{2,1,0:T(8,128)} copy(f32[8,32,128]{2,1,0:T(8,128)S(1)} %get-tuple-element.2) | data formatting | bytes 262144
  32.3 0.7 %copy.14 = f32[8,32,128]{2,1,0:T(8,128)} copy(f32[8,32,128]{2,1,0:T(8,128)S(1)} %get-tuple-element.3) | data formatting | bytes 262144

commit v3 on v2

--- a/solution.py
+++ b/solution.py
@@ -17,7 +17,20 @@
 AFFINE = BLK + NRHS
 WIDE = AFFINE + BLK
 ELEMENT = AFFINE + WIDE
-PIECES = ((0, AFFINE), (AFFINE, 2 * AFFINE), (2 * AFFINE, ELEMENT))
+CHIPS = 8
+FLOWS = (
+    (4, 0, 0, 1),
+    (4, 1, 0, 1),
+    (-3, 1, 0, 0),
+    (-3, 0, 0, 0),
+    (3, 0, 0, 2),
+    (3, 1, 0, 2),
+    (-2, 1, 1, 1),
+    (2, 0, 1, 0),
+    (-1, 1, 1, 0),
+    (1, 0, 1, 1),
+)
+PARTS_OF = ((0, AFFINE // 2), (AFFINE, WIDE // 2))
 
 
 def dot(left, right):
@@ -72,7 +85,9 @@
     bwd,
     bwd_values,
     pair,
-    ring,
+    whole,
+    far,
+    near,
     ends,
     last_own,
     last_in,
@@ -81,8 +96,9 @@
     load_sem,
     pair_send,
     pair_recv,
-    ring_send,
-    ring_recv,
+    flow_send,
+    far_recv,
+    near_recv,
     ends_send,
     ends_recv,
     last_send,
@@ -90,18 +106,12 @@
     rim_send,
     rim_recv,
 ):
-    chips = sections // 2
-    left_hops = chips // 2
-    right_hops = chips - 1 - left_hops
     section = lax.axis_index("section")
     part = lax.axis_index("dom")
     core = lax.rem(section, 2)
     chip = lax.div(section, 2)
     sibling = (section + 1 - 2 * core, part)
-    onto = (2 * lax.rem(chip + 1 - 2 * core + chips, chips) + core, part)
-    other = (2 * lax.rem(chip + 2 * core - 1 + chips, chips) + core, part)
     following = (lax.rem(section + 1, sections), part)
-    beyond = (lax.rem(section + 2 * core - 1 + sections, sections), part)
     part_up = (section, lax.min(part + 1, parts - 1))
     part_down = (section, lax.max(part - 1, 0))
 
@@ -121,7 +131,8 @@
         loads.append(copy)
 
     barrier = pltpu.get_barrier_semaphore()
-    for device in (sibling, onto, other, beyond):
+    for step in range(1, sections):
+        device = (lax.rem(section + step, sections), part)
         pl.semaphore_signal(barrier, inc=1, device_id=device, device_id_type=MESH)
 
     @pl.when(part < parts - 1)
@@ -139,6 +150,19 @@
     @pl.when(part == parts - 1)
     def _():
         rim[pl.ds(RIM, RIM)] = jnp.zeros((RIM, NRHS, BLK), BF16)
+
+    incoming = (
+        (far, far_recv, 0, chip + 3 < CHIPS),
+        (far, far_recv, 1, chip < 4),
+        (far, far_recv, 2, chip < 3),
+        (near, near_recv, 0, jnp.where(core == 0, chip < 2, chip + 1 < CHIPS)),
+        (near, near_recv, 1, jnp.where(core == 0, chip < 1, chip + 2 < CHIPS)),
+    )
+    for buffer, _, slot, full in incoming:
+
+        @pl.when(jnp.logical_not(full))
+        def _(buffer=buffer, slot=slot):
+            buffer[slot, AFFINE:] = jnp.zeros((WIDE, BLK), BF16)
 
     spread = lax.broadcasted_iota(jnp.int32, (BLK, BLK), 0)
     identity = (spread == lax.broadcasted_iota(jnp.int32, (BLK, BLK), 1)).astype(F32)
@@ -161,7 +185,7 @@
         fwd[k] = wide.astype(BF16)
     pair[core, :AFFINE] = fwd[ROWS - 1]
 
-    partners = 4 + (part < parts - 1).astype(jnp.int32) + (part > 0).astype(jnp.int32)
+    partners = sections - 1 + (part < parts - 1).astype(jnp.int32) + (part > 0).astype(jnp.int32)
     pl.semaphore_wait(barrier, partners)
 
     def pair_copy(piece, low, high):
@@ -203,59 +227,55 @@
     pair_onward.wait_recv()
     pair_back.wait_recv()
     onward, back = joined(pair[0], pair[1])
-    ring[0, :AFFINE] = onward
-    ring[0, AFFINE:] = back
-
-    def ring_copy(hop, piece):
-        low, high = PIECES[piece]
+    whole[:AFFINE] = onward
+    whole[AFFINE:] = back
+
+    def flow_copy(index, kind):
+        steps, target_core, buffer, slot = FLOWS[index]
+        target = (2 * lax.rem(chip + steps + CHIPS, CHIPS) + target_core, part)
+        low, size = PARTS_OF[kind]
+        place = pl.ds(pl.multiple_of(low + size * core, 16), size)
         return pltpu.make_async_remote_copy(
-            src_ref=ring.at[hop, pl.ds(low, high - low)],
-            dst_ref=ring.at[hop + 1, pl.ds(low, high - low)],
-            send_sem=ring_send.at[hop, piece],
-            recv_sem=ring_recv.at[hop, piece],
-            device_id=onto,
+            src_ref=whole.at[place],
+            dst_ref=(far, near)[buffer].at[slot, place],
+            send_sem=flow_send.at[index, kind],
+            recv_sem=(far_recv, near_recv)[buffer].at[slot, core, kind],
+            device_id=target,
             device_id_type=MESH,
         )
 
-    for piece in range(len(PIECES)):
-        ring_copy(0, piece).start()
-
-    def take(hop, last):
-        for piece in range(len(PIECES)):
-            ring_copy(hop - 1, piece).wait_recv()
-            if not last:
-                ring_copy(hop, piece).start()
-
-    def fold(hop, target, place):
-        done = 1 if hop == 2 else left_hops + 1
-        left = ring[jnp.where(core == 0, hop, done)]
-        right = ring[jnp.where(core == 0, done, hop)]
-        onward, back = joined(left, right)
-        target[place, :AFFINE] = onward
-        target[place, AFFINE:] = back
-
-    for hop in range(1, right_hops):
-        take(hop, False)
-        if hop >= 2:
-            fold(hop, ring, left_hops + 1)
-
-    @pl.when(core == 0)
-    def _():
-        for hop in range(right_hops, left_hops + 1):
-            take(hop, hop == left_hops)
-            if hop == left_hops:
-                fold(hop, ends, 0)
-            elif hop >= 2:
-                fold(hop, ring, left_hops + 1)
-
-    @pl.when(core == 1)
-    def _():
-        take(right_hops, True)
-        if right_hops >= 2:
-            fold(right_hops, ends, 1)
-        else:
-            ends[1] = ring[1]
-
+    def flow_full(index):
+        steps = FLOWS[index][0]
+        return chip + steps >= CHIPS if steps > 0 else chip + steps >= 0
+
+    for index in range(len(FLOWS)):
+        flow_copy(index, 0).start()
+        pl.when(flow_full(index))(flow_copy(index, 1).start)
+
+    def take(index):
+        buffer, sems, slot, full = incoming[index]
+
+        def landed(kind):
+            low, size = PARTS_OF[kind]
+            for half in range(2):
+                place = pl.ds(low + size * half, size)
+                pltpu.make_async_remote_copy(
+                    src_ref=whole.at[place],
+                    dst_ref=buffer.at[slot, place],
+                    send_sem=flow_send.at[0, kind],
+                    recv_sem=sems.at[slot, half, kind],
+                    device_id=sibling,
+                    device_id_type=MESH,
+                ).wait_recv()
+
+        landed(0)
+        pl.when(full)(functools.partial(landed, 1))
+
+    take(3)
+    take(4)
+    onward, back = joined(near[0], near[1])
+    ends[core, :AFFINE] = onward
+    ends[core, AFFINE:] = back
     ends_copy = pltpu.make_async_remote_copy(
         src_ref=ends.at[core],
         dst_ref=ends.at[core],
@@ -266,27 +286,34 @@
     )
     ends_copy.start()
     ends_copy.wait_recv()
-
-    def value(ref, place, low, size):
-        return ref[place, low : low + size]
-
-    inflow = value(ends, 0, BLK, NRHS).astype(F32) + dot(
-        value(ends, 1, BLK, NRHS), value(ends, 0, 0, BLK)
-    )
-    middle = value(pair, 0, BLK, NRHS).astype(F32) + dot(inflow, value(pair, 0, 0, BLK))
-    outgoing = value(pair, 1, BLK, NRHS).astype(F32) + dot(middle, value(pair, 1, 0, BLK))
-    far = value(ends, 1, BLK, NRHS).astype(F32) + dot(outgoing, value(ends, 1, 0, BLK))
-    near = dot(outgoing, value(ends, 1, AFFINE, BLK))
-    far = value(ends, 0, AFFINE + BLK, NRHS).astype(F32) + dot(far, value(ends, 0, AFFINE, BLK))
-    outflow = (
-        value(ends, 1, AFFINE + BLK, NRHS).astype(F32)
-        + near
-        + dot(far, value(ends, 1, 2 * AFFINE, BLK))
-    )
+    take(0)
+    ahead = jnp.concatenate(joined(ends[1], far[0]), axis=0)
+    take(2)
+    behind = jnp.concatenate(joined(far[2], ends[0]), axis=0)
+    take(1)
+    behind = jnp.concatenate(joined(far[1], behind), axis=0)
+
+    through = dot(
+        ahead[:AFFINE], jnp.concatenate([behind[:BLK], behind[AFFINE : AFFINE + BLK]], axis=1)
+    )
+    inflow = through[BLK:, :BLK] + behind[BLK:AFFINE].astype(F32)
+    back = jnp.concatenate(
+        [
+            through[:BLK, BLK:],
+            through[BLK:, BLK:] + behind[AFFINE + BLK : 2 * AFFINE].astype(F32),
+        ],
+        axis=0,
+    )
+    back = dot(back, ahead[2 * AFFINE :]) + ahead[AFFINE : 2 * AFFINE].astype(F32)
+    chip_maps = jnp.concatenate([whole[:BLK], pair[0, :BLK]], axis=1)
+    passed = dot(inflow, chip_maps)
+    outgoing = passed[:, :BLK] + whole[BLK:AFFINE].astype(F32)
+    middle = passed[:, BLK:] + pair[0, BLK:AFFINE].astype(F32)
+    outflow = back[BLK:] + dot(outgoing, back[:BLK].astype(BF16))
     centre = (
-        value(pair, 1, AFFINE + BLK, NRHS).astype(F32)
-        + dot(middle, value(pair, 1, AFFINE, BLK))
-        + dot(outflow, value(pair, 1, 2 * AFFINE, BLK))
+        pair[1, AFFINE + BLK : 2 * AFFINE].astype(F32)
+        + dot(middle, pair[1, AFFINE : AFFINE + BLK])
+        + dot(outflow, pair[1, 2 * AFFINE :])
     )
     inflow = jnp.where(core == 0, inflow, middle)
     outflow = jnp.where(core == 0, centre, outflow)
@@ -365,20 +392,12 @@
     def _():
         rim_copies[1].wait_send()
 
-    for hop in range(right_hops):
-        for piece in range(len(PIECES)):
-            ring_copy(hop, piece).wait_send()
-
-    @pl.when(core == 0)
-    def _():
-        for hop in range(right_hops, left_hops):
-            for piece in range(len(PIECES)):
-                ring_copy(hop, piece).wait_send()
+    for index in range(len(FLOWS)):
+        flow_copy(index, 0).wait_send()
+        pl.when(flow_full(index))(flow_copy(index, 1).wait_send)
 
 
 def on_device(sections, parts, rhs, inverse, diag, lower, upper, halo, low_index, up_index, halo_index):
-    chips = sections // 2
-    hops = chips // 2
     smem = pl.BlockSpec(memory_space=pltpu.SMEM)
     hbm = pl.BlockSpec(memory_space=pl.ANY)
     vmem = pl.BlockSpec(memory_space=pltpu.VMEM)
@@ -403,7 +422,9 @@
             pltpu.VMEM((ROWS + 1, WIDE, BLK), BF16),
             pltpu.VMEM((ROWS, NRHS, BLK), F32),
             pltpu.VMEM((2, ELEMENT, BLK), BF16),
-            pltpu.VMEM((hops + 2, ELEMENT, BLK), BF16),
+            pltpu.VMEM((ELEMENT, BLK), BF16),
+            pltpu.VMEM((3, ELEMENT, BLK), BF16),
+            pltpu.VMEM((2, ELEMENT, BLK), BF16),
             pltpu.VMEM((2, ELEMENT, BLK), BF16),
             pltpu.VMEM((BLK, BLK), BF16),
             pltpu.VMEM((BLK, BLK), BF16),
@@ -412,8 +433,9 @@
             dma((6,)),
             dma((2,)),
             dma((2,)),
-            dma((hops, len(PIECES))),
-            dma((hops, len(PIECES))),
+            dma((len(FLOWS), 2)),
+            dma((3, 2, 2)),
+            dma((2, 2, 2)),
             dma((1,)),
             dma((1,)),
             dma((1,)),

time: 33.1 us -> 39 us (1.18)
  Pallas kernels: 31 us -> 36.8 us
    pallas_call x1, Pallas kernels: 31 us -> 36.8 us  [on_device(): pl.pallas_call(functools.partial(kernel, sections, parts), out_shape=(plt...]
where the time goes in v3:
time: 39 us; the launch traced here: 38.8 us
  Pallas kernels  36.8 us (94%)
  local copies, waits for them, and re-layouts  1.31 us (3%)
  between operations  0.64 us (2%)
    pallas_call x1, Pallas kernels, on_device(): pl.pallas_call(functools.partial(kernel, sections, parts), out_shape=(plt...  36.8 us
    unnamed x2, local copies, waits for them, and re-layouts  1.31 us

profile of v3, /device:TPU:199, one launch (start us, length us, event | category | flops | bytes accessed | tf_op | source)
XLA Modules:
  0.0 38.8 jit_solution(10293747939958137230)
XLA Ops:
  0.6 36.8 %block_ilu_apply.1 = (f32[8,32,128]{2,1,0:T(8,128)S(1)}, f32[8,32,128]{2,1,0:T(8,128)S(1)}) custom-call(s32[3,8]{1,0:T(4,128)} %bitcast.3, s32[3,8]{1,0:T(4,128)} %bitcast.4, s32[2,8]{1,0:T(2,128)} %bitcast.5, f32[8,32,128]{2,1,0:T(8,128)} %rhs_hbm.1, bf16[8,128,128]{2,1,0:T(8,128)(2,1)} %inverse_hbm.1, bf16[8,128,128]{2,1,0:T(8,128)(2,1)} %diag_hbm.1, ...), custom_call_target="tpu_custom_call" | custom-call | tf_op jit(solution)/shard_map/block_ilu_apply/pallas_call | solution.py:405
  37.5 0.7 %copy.13 = f32[8,32,128]{2,1,0:T(8,128)} copy(f32[8,32,128]{2,1,0:T(8,128)S(1)} %get-tuple-element.2) | data formatting | bytes 262144
  38.1 0.7 %copy.14 = f32[8,32,128]{2,1,0:T(8,128)} copy(f32[8,32,128]{2,1,0:T(8,128)S(1)} %get-tuple-element.3) | data formatting | bytes 262144

commit v4 on v2

--- a/solution.py
+++ b/solution.py
@@ -17,7 +17,6 @@
 AFFINE = BLK + NRHS
 WIDE = AFFINE + BLK
 ELEMENT = AFFINE + WIDE
-PIECES = ((0, AFFINE), (AFFINE, 2 * AFFINE), (2 * AFFINE, ELEMENT))
 
 
 def dot(left, right):
@@ -72,8 +71,11 @@
     bwd,
     bwd_values,
     pair,
-    ring,
-    ends,
+    whole,
+    elements,
+    inflows,
+    outflows,
+    got,
     last_own,
     last_in,
     rows,
@@ -81,27 +83,26 @@
     load_sem,
     pair_send,
     pair_recv,
-    ring_send,
-    ring_recv,
-    ends_send,
-    ends_recv,
+    element_send,
+    element_recv,
+    result_send,
+    got_recv,
     last_send,
     last_recv,
     rim_send,
     rim_recv,
 ):
     chips = sections // 2
-    left_hops = chips // 2
-    right_hops = chips - 1 - left_hops
+    hub = chips // 2
     section = lax.axis_index("section")
     part = lax.axis_index("dom")
     core = lax.rem(section, 2)
     chip = lax.div(section, 2)
     sibling = (section + 1 - 2 * core, part)
-    onto = (2 * lax.rem(chip + 1 - 2 * core + chips, chips) + core, part)
-    other = (2 * lax.rem(chip + 2 * core - 1 + chips, chips) + core, part)
+    at_hub = section == 2 * hub
+    hub_device = (2 * hub, part)
+    beyond = (lax.rem(section + 2 * core - 1 + sections, sections), part)
     following = (lax.rem(section + 1, sections), part)
-    beyond = (lax.rem(section + 2 * core - 1 + sections, sections), part)
     part_up = (section, lax.min(part + 1, parts - 1))
     part_down = (section, lax.max(part - 1, 0))
 
@@ -121,9 +122,19 @@
         loads.append(copy)
 
     barrier = pltpu.get_barrier_semaphore()
-    for device in (sibling, onto, other, beyond):
+    for device in (sibling, beyond):
         pl.semaphore_signal(barrier, inc=1, device_id=device, device_id_type=MESH)
 
+    @pl.when(at_hub)
+    def _():
+        for other in range(sections):
+            if other != 2 * hub:
+                pl.semaphore_signal(barrier, inc=1, device_id=(other, part), device_id_type=MESH)
+
+    @pl.when(jnp.logical_not(at_hub))
+    def _():
+        pl.semaphore_signal(barrier, inc=1, device_id=hub_device, device_id_type=MESH)
+
     @pl.when(part < parts - 1)
     def _():
         pl.semaphore_signal(barrier, inc=1, device_id=part_up, device_id_type=MESH)
@@ -139,6 +150,14 @@
     @pl.when(part == parts - 1)
     def _():
         rim[pl.ds(RIM, RIM)] = jnp.zeros((RIM, NRHS, BLK), BF16)
+
+    @pl.when(chip == 0)
+    def _():
+        got[0] = jnp.zeros((NRHS, BLK), BF16)
+
+    @pl.when(chip == chips - 1)
+    def _():
+        got[1] = jnp.zeros((NRHS, BLK), BF16)
 
     spread = lax.broadcasted_iota(jnp.int32, (BLK, BLK), 0)
     identity = (spread == lax.broadcasted_iota(jnp.int32, (BLK, BLK), 1)).astype(F32)
@@ -161,7 +180,7 @@
         fwd[k] = wide.astype(BF16)
     pair[core, :AFFINE] = fwd[ROWS - 1]
 
-    partners = 4 + (part < parts - 1).astype(jnp.int32) + (part > 0).astype(jnp.int32)
+    partners = jnp.where(at_hub, sections + 1, 3) + (part < parts - 1).astype(jnp.int32) + (part > 0).astype(jnp.int32)
     pl.semaphore_wait(barrier, partners)
 
     def pair_copy(piece, low, high):
@@ -203,91 +222,109 @@
     pair_onward.wait_recv()
     pair_back.wait_recv()
     onward, back = joined(pair[0], pair[1])
-    ring[0, :AFFINE] = onward
-    ring[0, AFFINE:] = back
-
-    def ring_copy(hop, piece):
-        low, high = PIECES[piece]
+    whole[:AFFINE] = onward
+    whole[AFFINE:] = back
+
+    def element_copy(origin, half, low, rows_sent):
+        place = pl.ds(pl.multiple_of(low + rows_sent * half, 16), rows_sent)
         return pltpu.make_async_remote_copy(
-            src_ref=ring.at[hop, pl.ds(low, high - low)],
-            dst_ref=ring.at[hop + 1, pl.ds(low, high - low)],
-            send_sem=ring_send.at[hop, piece],
-            recv_sem=ring_recv.at[hop, piece],
-            device_id=onto,
+            src_ref=whole.at[place],
+            dst_ref=elements.at[origin, place],
+            send_sem=element_send.at[0],
+            recv_sem=element_recv.at[origin, half],
+            device_id=hub_device,
             device_id_type=MESH,
         )
 
-    for piece in range(len(PIECES)):
-        ring_copy(0, piece).start()
-
-    def take(hop, last):
-        for piece in range(len(PIECES)):
-            ring_copy(hop - 1, piece).wait_recv()
-            if not last:
-                ring_copy(hop, piece).start()
-
-    def fold(hop, target, place):
-        done = 1 if hop == 2 else left_hops + 1
-        left = ring[jnp.where(core == 0, hop, done)]
-        right = ring[jnp.where(core == 0, done, hop)]
-        onward, back = joined(left, right)
-        target[place, :AFFINE] = onward
-        target[place, AFFINE:] = back
-
-    for hop in range(1, right_hops):
-        take(hop, False)
-        if hop >= 2:
-            fold(hop, ring, left_hops + 1)
-
-    @pl.when(core == 0)
-    def _():
-        for hop in range(right_hops, left_hops + 1):
-            take(hop, hop == left_hops)
-            if hop == left_hops:
-                fold(hop, ends, 0)
-            elif hop >= 2:
-                fold(hop, ring, left_hops + 1)
-
-    @pl.when(core == 1)
-    def _():
-        take(right_hops, True)
-        if right_hops >= 2:
-            fold(right_hops, ends, 1)
-        else:
-            ends[1] = ring[1]
-
-    ends_copy = pltpu.make_async_remote_copy(
-        src_ref=ends.at[core],
-        dst_ref=ends.at[core],
-        send_sem=ends_send.at[0],
-        recv_sem=ends_recv.at[0],
-        device_id=sibling,
-        device_id_type=MESH,
-    )
-    ends_copy.start()
-    ends_copy.wait_recv()
-
-    def value(ref, place, low, size):
-        return ref[place, low : low + size]
-
-    inflow = value(ends, 0, BLK, NRHS).astype(F32) + dot(
-        value(ends, 1, BLK, NRHS), value(ends, 0, 0, BLK)
-    )
-    middle = value(pair, 0, BLK, NRHS).astype(F32) + dot(inflow, value(pair, 0, 0, BLK))
-    outgoing = value(pair, 1, BLK, NRHS).astype(F32) + dot(middle, value(pair, 1, 0, BLK))
-    far = value(ends, 1, BLK, NRHS).astype(F32) + dot(outgoing, value(ends, 1, 0, BLK))
-    near = dot(outgoing, value(ends, 1, AFFINE, BLK))
-    far = value(ends, 0, AFFINE + BLK, NRHS).astype(F32) + dot(far, value(ends, 0, AFFINE, BLK))
-    outflow = (
-        value(ends, 1, AFFINE + BLK, NRHS).astype(F32)
-        + near
-        + dot(far, value(ends, 1, 2 * AFFINE, BLK))
-    )
-    centre = (
-        value(pair, 1, AFFINE + BLK, NRHS).astype(F32)
-        + dot(middle, value(pair, 1, AFFINE, BLK))
-        + dot(outflow, value(pair, 1, 2 * AFFINE, BLK))
-    )
+    def extent(origin):
+        if origin == 0:
+            return BLK, NRHS // 2
+        if origin == chips - 1:
+            return AFFINE, AFFINE // 2
+        return 0, ELEMENT // 2
+
+    groups = (
+        (chip == 0, 0),
+        (chip == chips - 1, chips - 1),
+        ((chip > 0) & (chip < chips - 1) & (chip != hub), 1),
+    )
+    for member, kind in groups:
+
+        @pl.when(member)
+        def _(kind=kind):
+            element_copy(chip, core, *extent(kind)).start()
+
+    def result_copy(kind, target, target_core):
+        return pltpu.make_async_remote_copy(
+            src_ref=(inflows, outflows)[kind].at[target],
+            dst_ref=got.at[kind],
+            send_sem=result_send.at[target, kind, target_core],
+            recv_sem=got_recv.at[kind],
+            device_id=(2 * target + target_core, part),
+            device_id_type=MESH,
+        )
+
+    def result_copies(kind, target):
+        return [
+            result_copy(kind, target, target_core)
+            for target_core in (1, 0)
+            if (target, target_core) != (hub, 0)
+        ]
+
+    @pl.when(at_hub)
+    def _():
+        def take(origin):
+            for half in range(2):
+                element_copy(origin, half, *extent(origin)).wait_recv()
+
+        def part_of(origin, low, size):
+            ref = whole if origin == hub else elements.at[origin]
+            return ref[low : low + size]
+
+        running = None
+        for origin in range(chips):
+            if origin > 0:
+                inflows[origin] = running.astype(BF16)
+                for copy in result_copies(0, origin):
+                    copy.start()
+            if origin != hub:
+                take(origin)
+            if origin < chips - 1:
+                values = part_of(origin, BLK, NRHS).astype(F32)
+                if origin > 0:
+                    values = values + dot(running, part_of(origin, 0, BLK))
+                running = values
+        running = None
+        for origin in range(chips - 1, 0, -1):
+            values = part_of(origin, AFFINE + BLK, NRHS).astype(F32)
+            values = values + dot(inflows[origin], part_of(origin, AFFINE, BLK))
+            if origin < chips - 1:
+                values = values + dot(running, part_of(origin, 2 * AFFINE, BLK))
+            running = values
+            outflows[origin - 1] = running.astype(BF16)
+        for target in range(chips - 1):
+            target = (target + 1) // 2 if target % 2 == 0 else chips - 1 - (target + 1) // 2
+            for copy in result_copies(1, target):
+                copy.start()
+        got[0] = inflows[hub]
+        got[1] = outflows[hub]
+
+    @pl.when(jnp.logical_not(at_hub) & (chip > 0))
+    def _():
+        result_copy(0, 1, 0).wait_recv()
+
+    inflow = got[0].astype(F32)
+    middle = dot(inflow, pair[0, :BLK]) + pair[0, BLK:AFFINE].astype(F32)
+    centre = pair[1, AFFINE + BLK : 2 * AFFINE].astype(F32) + dot(
+        middle, pair[1, AFFINE : AFFINE + BLK]
+    )
+
+    @pl.when(jnp.logical_not(at_hub) & (chip < chips - 1))
+    def _():
+        result_copy(1, 1, 0).wait_recv()
+
+    outflow = got[1].astype(F32)
+    centre = centre + dot(got[1], pair[1, 2 * AFFINE :])
     inflow = jnp.where(core == 0, inflow, middle)
     outflow = jnp.where(core == 0, centre, outflow)
     flows = jnp.concatenate([inflow, outflow], axis=1).astype(BF16)
@@ -355,7 +392,6 @@
     pair_onward.wait_send()
     pair_back.wait_send()
     last_copy.wait_send()
-    ends_copy.wait_send()
 
     @pl.when(part < parts - 1)
     def _():
@@ -365,20 +401,22 @@
     def _():
         rim_copies[1].wait_send()
 
-    for hop in range(right_hops):
-        for piece in range(len(PIECES)):
-            ring_copy(hop, piece).wait_send()
-
-    @pl.when(core == 0)
-    def _():
-        for hop in range(right_hops, left_hops):
-            for piece in range(len(PIECES)):
-                ring_copy(hop, piece).wait_send()
+    for member, kind in groups:
+
+        @pl.when(member)
+        def _(kind=kind):
+            element_copy(chip, core, *extent(kind)).wait_send()
+
+    @pl.when(at_hub)
+    def _():
+        for kind in range(2):
+            for target in range(1 - kind, chips - kind):
+                for copy in result_copies(kind, target):
+                    copy.wait_send()
 
 
 def on_device(sections, parts, rhs, inverse, diag, lower, upper, halo, low_index, up_index, halo_index):
     chips = sections // 2
-    hops = chips // 2
     smem = pl.BlockSpec(memory_space=pltpu.SMEM)
     hbm = pl.BlockSpec(memory_space=pl.ANY)
     vmem = pl.BlockSpec(memory_space=pltpu.VMEM)
@@ -403,8 +441,11 @@
             pltpu.VMEM((ROWS + 1, WIDE, BLK), BF16),
             pltpu.VMEM((ROWS, NRHS, BLK), F32),
             pltpu.VMEM((2, ELEMENT, BLK), BF16),
-            pltpu.VMEM((hops + 2, ELEMENT, BLK), BF16),
-            pltpu.VMEM((2, ELEMENT, BLK), BF16),
+            pltpu.VMEM((ELEMENT, BLK), BF16),
+            pltpu.VMEM((chips, ELEMENT, BLK), BF16),
+            pltpu.VMEM((chips, NRHS, BLK), BF16),
+            pltpu.VMEM((chips, NRHS, BLK), BF16),
+            pltpu.VMEM((2, NRHS, BLK), BF16),
             pltpu.VMEM((BLK, BLK), BF16),
             pltpu.VMEM((BLK, BLK), BF16),
             pltpu.VMEM((ROWS + 2, NRHS, BLK), BF16),
@@ -412,10 +453,10 @@
             dma((6,)),
             dma((2,)),
             dma((2,)),
-            dma((hops, len(PIECES))),
-            dma((hops, len(PIECES))),
             dma((1,)),
-            dma((1,)),
+            dma((chips, 2)),
+            dma((chips, 2, 2)),
+            dma((2,)),
             dma((1,)),
             dma((1,)),
             dma((2,)),

time: 33.1 us -> 30.4 us (0.918)
  the two profiles are of different devices: /device:TPU:199 before, /device:TPU:198 now
where the time goes in v4:
time: 30.4 us; the launch traced here: 30.2 us
  Pallas kernels  28.2 us (93%)
  local copies, waits for them, and re-layouts  1.31 us (4%)
  between operations  0.64 us (2%)
    pallas_call x1, Pallas kernels, on_device(): pl.pallas_call(functools.partial(kernel, sections, parts), out_shape=(plt...  28.2 us
    unnamed x2, local copies, waits for them, and re-layouts  1.31 us

profile of v4, /device:TPU:198, one launch (start us, length us, event | category | flops | bytes accessed | tf_op | source)
XLA Modules:
  0.0 30.2 jit_solution(6703706529040981619)
XLA Ops:
  0.6 28.2 %block_ilu_apply.1 = (f32[8,32,128]{2,1,0:T(8,128)S(1)}, f32[8,32,128]{2,1,0:T(8,128)S(1)}) custom-call(s32[3,8]{1,0:T(4,128)} %bitcast.3, s32[3,8]{1,0:T(4,128)} %bitcast.4, s32[2,8]{1,0:T(2,128)} %bitcast.5, f32[8,32,128]{2,1,0:T(8,128)} %rhs_hbm.1, bf16[8,128,128]{2,1,0:T(8,128)(2,1)} %inverse_hbm.1, bf16[8,128,128]{2,1,0:T(8,128)(2,1)} %diag_hbm.1, ...), custom_call_target="tpu_custom_call" | custom-call | tf_op jit(solution)/shard_map/block_ilu_apply/pallas_call | solution.py:424
  28.9 0.7 %copy.13 = f32[8,32,128]{2,1,0:T(8,128)} copy(f32[8,32,128]{2,1,0:T(8,128)S(1)} %get-tuple-element.2) | data formatting | bytes 262144
  29.5 0.7 %copy.14 = f32[8,32,128]{2,1,0:T(8,128)} copy(f32[8,32,128]{2,1,0:T(8,128)S(1)} %get-tuple-element.3) | data formatting | bytes 262144

commit v5 on v4

--- a/solution.py
+++ b/solution.py
@@ -49,9 +49,9 @@
 def kernel(
     sections,
     parts,
-    lower_index,
-    upper_index,
-    halo_index,
+    lower_index_hbm,
+    upper_index_hbm,
+    halo_index_hbm,
     rhs_hbm,
     inverse_hbm,
     diag_hbm,
@@ -60,6 +60,9 @@
     halo_hbm,
     solution_ref,
     product_ref,
+    lower_index,
+    upper_index,
+    halo_index,
     rhs,
     inverse,
     diag,
@@ -93,14 +96,14 @@
     rim_recv,
 ):
     chips = sections // 2
-    hub = chips // 2
+    middle_chip = chips // 2
     section = lax.axis_index("section")
     part = lax.axis_index("dom")
     core = lax.rem(section, 2)
     chip = lax.div(section, 2)
     sibling = (section + 1 - 2 * core, part)
-    at_hub = section == 2 * hub
-    hub_device = (2 * hub, part)
+    at_hub = section == 1
+    hub_device = (1, part)
     beyond = (lax.rem(section + 2 * core - 1 + sections, sections), part)
     following = (lax.rem(section + 1, sections), part)
     part_up = (section, lax.min(part + 1, parts - 1))
@@ -109,10 +112,13 @@
     loads = []
     for place, (source, target) in enumerate(
         (
+            (lower_index_hbm, lower_index),
             (lower_hbm, lower),
             (inverse_hbm, inverse),
             (rhs_hbm, rhs),
+            (upper_index_hbm, upper_index),
             (upper_hbm, upper),
+            (halo_index_hbm, halo_index),
             (diag_hbm, diag),
             (halo_hbm, halo),
         )
@@ -128,7 +134,7 @@
     @pl.when(at_hub)
     def _():
         for other in range(sections):
-            if other != 2 * hub:
+            if other != 1:
                 pl.semaphore_signal(barrier, inc=1, device_id=(other, part), device_id_type=MESH)
 
     @pl.when(jnp.logical_not(at_hub))
@@ -168,7 +174,7 @@
     bwd[ROWS, :AFFINE] = jnp.zeros((AFFINE, BLK), BF16)
     bwd[ROWS, AFFINE:] = (identity * has_after).astype(BF16)
 
-    for copy in loads[:3]:
+    for copy in loads[:4]:
         copy.wait()
     for k in range(ROWS):
         folded = dot(lower[k].reshape(3 * BLK, BLK), inverse[k])
@@ -197,7 +203,8 @@
     pair_back = pair_copy(1, AFFINE, ELEMENT)
     pair_onward.start()
 
-    loads[3].wait()
+    for copy in loads[4:6]:
+        copy.wait()
     for k in range(ROWS - 1, -1, -1):
         folded = dot(upper[k].reshape(3 * BLK, BLK), inverse[k])
         if k == ROWS - 1:
@@ -237,16 +244,11 @@
         )
 
     def extent(origin):
-        if origin == 0:
-            return BLK, NRHS // 2
-        if origin == chips - 1:
-            return AFFINE, AFFINE // 2
-        return 0, ELEMENT // 2
+        return (AFFINE, AFFINE // 2) if origin == chips - 1 else (0, ELEMENT // 2)
 
     groups = (
-        (chip == 0, 0),
         (chip == chips - 1, chips - 1),
-        ((chip > 0) & (chip < chips - 1) & (chip != hub), 1),
+        ((chip > 0) & (chip < chips - 1), 1),
     )
     for member, kind in groups:
 
@@ -267,8 +269,8 @@
     def result_copies(kind, target):
         return [
             result_copy(kind, target, target_core)
-            for target_core in (1, 0)
-            if (target, target_core) != (hub, 0)
+            for target_core in (0, 1)
+            if (target, target_core) != (0, 1)
         ]
 
     @pl.when(at_hub)
@@ -278,36 +280,61 @@
                 element_copy(origin, half, *extent(origin)).wait_recv()
 
         def part_of(origin, low, size):
-            ref = whole if origin == hub else elements.at[origin]
+            ref = elements.at[origin] if origin else whole
             return ref[low : low + size]
 
+        def onward(origin, running):
+            values = part_of(origin, BLK, NRHS).astype(F32)
+            return values + dot(running, part_of(origin, 0, BLK)) if origin else values
+
+        def give(kind, target, values):
+            (inflows, outflows)[kind][target] = values.astype(BF16)
+            for copy in result_copies(kind, target):
+                copy.start()
+
+        for origin in sorted(range(1, chips), key=lambda c: min(c, chips - c)):
+            if origin != middle_chip:
+                take(origin)
         running = None
-        for origin in range(chips):
-            if origin > 0:
-                inflows[origin] = running.astype(BF16)
-                for copy in result_copies(0, origin):
-                    copy.start()
-            if origin != hub:
-                take(origin)
-            if origin < chips - 1:
-                values = part_of(origin, BLK, NRHS).astype(F32)
-                if origin > 0:
-                    values = values + dot(running, part_of(origin, 0, BLK))
-                running = values
-        running = None
-        for origin in range(chips - 1, 0, -1):
-            values = part_of(origin, AFFINE + BLK, NRHS).astype(F32)
-            values = values + dot(inflows[origin], part_of(origin, AFFINE, BLK))
-            if origin < chips - 1:
-                values = values + dot(running, part_of(origin, 2 * AFFINE, BLK))
-            running = values
-            outflows[origin - 1] = running.astype(BF16)
-        for target in range(chips - 1):
-            target = (target + 1) // 2 if target % 2 == 0 else chips - 1 - (target + 1) // 2
-            for copy in result_copies(1, target):
-                copy.start()
-        got[0] = inflows[hub]
-        got[1] = outflows[hub]
+        known = [None] * chips
+        for origin in range(middle_chip):
+            running = onward(origin, running)
+            give(0, origin + 1, running)
+            if origin:
+                known[origin] = part_of(origin, AFFINE + BLK, NRHS).astype(F32) + dot(
+                    inflows[origin], part_of(origin, AFFINE, BLK)
+                )
+        runs = [None] * chips
+        runs[-1] = part_of(chips - 1, AFFINE, AFFINE)
+        for origin in range(chips - 2, middle_chip, -1):
+            spread_b = jnp.concatenate(
+                [jnp.zeros((BLK, BLK), F32), runs[origin + 1][BLK:].astype(F32)], axis=0
+            )
+            through = dot(part_of(origin, 0, AFFINE), runs[origin + 1][:BLK]) + spread_b
+            through = dot(through, part_of(origin, 2 * AFFINE, BLK))
+            runs[origin] = (through + part_of(origin, AFFINE, AFFINE).astype(F32)).astype(BF16)
+        take(middle_chip)
+        known[middle_chip] = part_of(middle_chip, AFFINE + BLK, NRHS).astype(F32) + dot(
+            inflows[middle_chip], part_of(middle_chip, AFFINE, BLK)
+        )
+
+        def returned(origin, running):
+            return runs[origin + 1][BLK:].astype(F32) + dot(running, runs[origin + 1][:BLK])
+
+        running = onward(middle_chip, running)
+        back = returned(middle_chip, running)
+        give(1, middle_chip, back)
+        give(0, middle_chip + 1, running)
+        for origin in range(middle_chip, 0, -1):
+            back = known[origin] + dot(back, part_of(origin, 2 * AFFINE, BLK))
+            give(1, origin - 1, back)
+            ahead = 2 * middle_chip - origin + 1
+            if ahead < chips:
+                running = onward(ahead, running) if ahead < chips - 1 else running
+                if ahead < chips - 1:
+                    give(1, ahead, returned(ahead, running))
+                    give(0, ahead + 1, running)
+        got[1] = outflows[0]
 
     @pl.when(jnp.logical_not(at_hub) & (chip > 0))
     def _():
@@ -364,7 +391,7 @@
     edges_before = (inflow - dot(rows[0], last_in[...])) * has_before
     edges = jnp.stack([edges_before, outflow * has_after]).astype(BF16)
     rows[pl.ds(ROWS, 2)] = edges
-    for copy in loads[4:]:
+    for copy in loads[6:]:
         copy.wait()
     totals = []
     for k in range(ROWS):
@@ -417,7 +444,6 @@
 
 def on_device(sections, parts, rhs, inverse, diag, lower, upper, halo, low_index, up_index, halo_index):
     chips = sections // 2
-    smem = pl.BlockSpec(memory_space=pltpu.SMEM)
     hbm = pl.BlockSpec(memory_space=pl.ANY)
     vmem = pl.BlockSpec(memory_space=pltpu.VMEM)
     dma = pltpu.SemaphoreType.DMA
@@ -427,9 +453,12 @@
             pltpu.VMEM(rhs.shape, F32),
             pltpu.VMEM(rhs.shape, F32),
         ),
-        in_specs=[smem] * 3 + [hbm] * 6,
+        in_specs=[hbm] * 9,
         out_specs=(vmem, vmem),
         scratch_shapes=[
+            pltpu.SMEM(low_index.T.shape, jnp.int32),
+            pltpu.SMEM(up_index.T.shape, jnp.int32),
+            pltpu.SMEM(halo_index.T.shape, jnp.int32),
             pltpu.VMEM(rhs.shape, F32),
             pltpu.VMEM(inverse.shape, BF16),
             pltpu.VMEM(diag.shape, BF16),
@@ -450,7 +479,7 @@
             pltpu.VMEM((BLK, BLK), BF16),
             pltpu.VMEM((ROWS + 2, NRHS, BLK), BF16),
             pltpu.VMEM((2 * RIM, NRHS, BLK), BF16),
-            dma((6,)),
+            dma((9,)),
             dma((2,)),
             dma((2,)),
             dma((1,)),

time: 30.4 us -> 27.6 us (0.908)
  the two profiles are of different devices: /device:TPU:198 before, /device:TPU:206 now
where the time goes in v5:
time: 27.6 us; the launch traced here: 27.4 us
  Pallas kernels  25.5 us (92%)
  local copies, waits for them, and re-layouts  1.31 us (5%)
  between operations  0.64 us (2%)
    pallas_call x1, Pallas kernels, on_device(): pl.pallas_call(functools.partial(kernel, sections, parts), out_shape=(plt...  25.5 us
    unnamed x2, local copies, waits for them, and re-layouts  1.31 us

profile of v5, /device:TPU:206, one launch (start us, length us, event | category | flops | bytes accessed | tf_op | source)
XLA Modules:
  0.0 27.4 jit_solution(16546924699422960188)
XLA Ops:
  0.6 25.5 %block_ilu_apply.1 = (f32[8,32,128]{2,1,0:T(8,128)S(1)}, f32[8,32,128]{2,1,0:T(8,128)S(1)}) custom-call(s32[3,8]{1,0:T(4,128)} %bitcast.3, s32[3,8]{1,0:T(4,128)} %bitcast.4, s32[2,8]{1,0:T(2,128)} %bitcast.5, f32[8,32,128]{2,1,0:T(8,128)} %rhs_hbm.1, bf16[8,128,128]{2,1,0:T(8,128)(2,1)} %inverse_hbm.1, bf16[8,128,128]{2,1,0:T(8,128)(2,1)} %diag_hbm.1, ...), custom_call_target="tpu_custom_call" | custom-call | tf_op jit(solution)/shard_map/block_ilu_apply/pallas_call | solution.py:450
  26.1 0.7 %copy.13 = f32[8,32,128]{2,1,0:T(8,128)} copy(f32[8,32,128]{2,1,0:T(8,128)S(1)} %get-tuple-element.2) | data formatting | bytes 262144
  26.8 0.7 %copy.14 = f32[8,32,128]{2,1,0:T(8,128)} copy(f32[8,32,128]{2,1,0:T(8,128)S(1)} %get-tuple-element.3) | data formatting | bytes 262144

commit v6 on v5

--- a/solution.py
+++ b/solution.py
@@ -23,27 +23,24 @@
     return jnp.dot(left.astype(BF16), right, preferred_element_type=F32)
 
 
-def joined(left, right):
-    right_m, right_a = right[:BLK], right[BLK:AFFINE]
-    right_h, right_b = right[AFFINE : AFFINE + BLK], right[AFFINE + BLK : 2 * AFFINE]
-    right_k, left_k = right[2 * AFFINE :], left[2 * AFFINE :]
-    through = dot(left[:AFFINE], jnp.concatenate([right_m, right_h], axis=1))
-    onward = jnp.concatenate(
-        [through[:BLK, :BLK], through[BLK:, :BLK] + right_a.astype(F32)], axis=0
-    )
-    back = jnp.concatenate(
-        [
-            through[:BLK, BLK:].astype(BF16),
-            (through[BLK:, BLK:] + right_b.astype(F32)).astype(BF16),
-            right_k,
-        ],
-        axis=0,
-    )
-    back = dot(back, left_k)
-    back = jnp.concatenate(
-        [back[:AFFINE] + left[AFFINE : 2 * AFFINE].astype(F32), back[AFFINE:]], axis=0
-    )
-    return onward.astype(BF16), back.astype(BF16)
+def joined_onward(left, right):
+    through = dot(left[:AFFINE], right[:BLK])
+    return jnp.concatenate(
+        [through[:BLK], through[BLK:] + right[BLK:AFFINE].astype(F32)], axis=0
+    ).astype(BF16)
+
+
+def joined_back(onward, back, right):
+    through = dot(onward, right[:BLK])
+    through = [through[:BLK], through[BLK:] + right[BLK:AFFINE].astype(F32)]
+    through = [part.astype(BF16) for part in through]
+    if right.shape[0] > AFFINE:
+        through.append(right[AFFINE:])
+    through = dot(jnp.concatenate(through, axis=0), back[AFFINE:])
+    affine = through[:AFFINE] + back[:AFFINE].astype(F32)
+    if right.shape[0] == AFFINE:
+        return affine.astype(BF16)
+    return jnp.concatenate([affine, through[AFFINE:]], axis=0).astype(BF16)
 
 
 def kernel(
@@ -226,35 +223,38 @@
         bwd[k] = wide.astype(BF16)
     pair[core, AFFINE:] = bwd[0]
     pair_back.start()
-    pair_onward.wait_recv()
-    pair_back.wait_recv()
-    onward, back = joined(pair[0], pair[1])
-    whole[:AFFINE] = onward
-    whole[AFFINE:] = back
-
-    def element_copy(origin, half, low, rows_sent):
-        place = pl.ds(pl.multiple_of(low + rows_sent * half, 16), rows_sent)
+
+    def element_copy(origin, half, kind, low, size):
+        place = pl.ds(pl.multiple_of(low + size * half, 16), size)
         return pltpu.make_async_remote_copy(
             src_ref=whole.at[place],
             dst_ref=elements.at[origin, place],
-            send_sem=element_send.at[0],
-            recv_sem=element_recv.at[origin, half],
+            send_sem=element_send.at[kind],
+            recv_sem=element_recv.at[origin, half, kind],
             device_id=hub_device,
             device_id_type=MESH,
         )
 
-    def extent(origin):
-        return (AFFINE, AFFINE // 2) if origin == chips - 1 else (0, ELEMENT // 2)
-
-    groups = (
-        (chip == chips - 1, chips - 1),
-        ((chip > 0) & (chip < chips - 1), 1),
-    )
-    for member, kind in groups:
-
-        @pl.when(member)
-        def _(kind=kind):
-            element_copy(chip, core, *extent(kind)).start()
+    def extent(kind, last):
+        if kind == 0:
+            return 0, AFFINE // 2
+        return AFFINE, AFFINE // 2 if last else WIDE // 2
+
+    between = (chip > 0) & (chip < chips - 1)
+    groups = ((between, 0, False), (between, 1, False), (chip == chips - 1, 1, True))
+
+    def send_element(wanted, action):
+        for member, kind, last in groups:
+            if kind == wanted:
+                copy = element_copy(chip, core, kind, *extent(kind, last))
+                pl.when(member)(getattr(copy, action))
+
+    pair_onward.wait_recv()
+    whole[:AFFINE] = joined_onward(pair[0, :AFFINE], pair[1, :AFFINE])
+    send_element(0, "start")
+    pair_back.wait_recv()
+    whole[AFFINE:] = joined_back(pair[0, :AFFINE], pair[0, AFFINE:], pair[1, AFFINE:])
+    send_element(1, "start")
 
     def result_copy(kind, target, target_core):
         return pltpu.make_async_remote_copy(
@@ -275,9 +275,11 @@
 
     @pl.when(at_hub)
     def _():
-        def take(origin):
-            for half in range(2):
-                element_copy(origin, half, *extent(origin)).wait_recv()
+        def take(origin, kind):
+            last = origin == chips - 1
+            if kind == 1 or not last:
+                for half in range(2):
+                    element_copy(origin, half, kind, *extent(kind, last)).wait_recv()
 
         def part_of(origin, low, size):
             ref = elements.at[origin] if origin else whole
@@ -292,48 +294,47 @@
             for copy in result_copies(kind, target):
                 copy.start()
 
-        for origin in sorted(range(1, chips), key=lambda c: min(c, chips - c)):
-            if origin != middle_chip:
-                take(origin)
+        order = sorted(range(1, chips), key=lambda c: min(c, chips - c))
+        for origin in order:
+            take(origin, 0)
         running = None
-        known = [None] * chips
-        for origin in range(middle_chip):
+        for origin in range(chips - 1):
             running = onward(origin, running)
             give(0, origin + 1, running)
-            if origin:
-                known[origin] = part_of(origin, AFFINE + BLK, NRHS).astype(F32) + dot(
-                    inflows[origin], part_of(origin, AFFINE, BLK)
-                )
+        for origin in order[:-1]:
+            take(origin, 1)
         runs = [None] * chips
         runs[-1] = part_of(chips - 1, AFFINE, AFFINE)
         for origin in range(chips - 2, middle_chip, -1):
-            spread_b = jnp.concatenate(
-                [jnp.zeros((BLK, BLK), F32), runs[origin + 1][BLK:].astype(F32)], axis=0
+            runs[origin] = joined_back(
+                part_of(origin, 0, AFFINE), part_of(origin, AFFINE, WIDE), runs[origin + 1]
             )
-            through = dot(part_of(origin, 0, AFFINE), runs[origin + 1][:BLK]) + spread_b
-            through = dot(through, part_of(origin, 2 * AFFINE, BLK))
-            runs[origin] = (through + part_of(origin, AFFINE, AFFINE).astype(F32)).astype(BF16)
-        take(middle_chip)
-        known[middle_chip] = part_of(middle_chip, AFFINE + BLK, NRHS).astype(F32) + dot(
-            inflows[middle_chip], part_of(middle_chip, AFFINE, BLK)
+        for origin in range(middle_chip, chips - 1):
+            beyond_run = runs[origin + 1]
+            outflow = beyond_run[BLK:].astype(F32) + dot(inflows[origin + 1], beyond_run[:BLK])
+            give(1, origin, outflow)
+        shifts = [None] * chips
+        gains = [None] * chips
+        for origin in range(middle_chip - 1, 0, -1):
+            shift = part_of(origin, AFFINE + BLK, NRHS).astype(F32) + dot(
+                inflows[origin], part_of(origin, AFFINE, BLK)
+            )
+            gain = part_of(origin, 2 * AFFINE, BLK)
+            if origin < middle_chip - 1:
+                shift = shift + dot(shifts[origin + 1], gain)
+                gain = dot(gains[origin + 1], gain).astype(BF16)
+            shifts[origin], gains[origin] = shift, gain
+
+        take(middle_chip, 1)
+        first = part_of(middle_chip, AFFINE + BLK, NRHS).astype(F32) + dot(
+            jnp.concatenate([inflows[middle_chip], outflows[middle_chip]], axis=1),
+            jnp.concatenate(
+                [part_of(middle_chip, AFFINE, BLK), part_of(middle_chip, 2 * AFFINE, BLK)], axis=0
+            ),
         )
-
-        def returned(origin, running):
-            return runs[origin + 1][BLK:].astype(F32) + dot(running, runs[origin + 1][:BLK])
-
-        running = onward(middle_chip, running)
-        back = returned(middle_chip, running)
-        give(1, middle_chip, back)
-        give(0, middle_chip + 1, running)
-        for origin in range(middle_chip, 0, -1):
-            back = known[origin] + dot(back, part_of(origin, 2 * AFFINE, BLK))
-            give(1, origin - 1, back)
-            ahead = 2 * middle_chip - origin + 1
-            if ahead < chips:
-                running = onward(ahead, running) if ahead < chips - 1 else running
-                if ahead < chips - 1:
-                    give(1, ahead, returned(ahead, running))
-                    give(0, ahead + 1, running)
+        give(1, middle_chip - 1, first)
+        for origin in range(middle_chip - 1, 0, -1):
+            give(1, origin - 1, shifts[origin] + dot(first, gains[origin]))
         got[1] = outflows[0]
 
     @pl.when(jnp.logical_not(at_hub) & (chip > 0))
@@ -428,11 +429,8 @@
     def _():
         rim_copies[1].wait_send()
 
-    for member, kind in groups:
-
-        @pl.when(member)
-        def _(kind=kind):
-            element_copy(chip, core, *extent(kind)).wait_send()
+    for kind in range(2):
+        send_element(kind, "wait_send")
 
     @pl.when(at_hub)
     def _():
@@ -440,6 +438,17 @@
             for target in range(1 - kind, chips - kind):
                 for copy in result_copies(kind, target):
                     copy.wait_send()
+
+
+def store(solved, product, solution_ref, product_ref, sems):
+    copies = [
+        pltpu.make_async_copy(solved, solution_ref, sems.at[0]),
+        pltpu.make_async_copy(product, product_ref, sems.at[1]),
+    ]
+    for copy in copies:
+        copy.start()
+    for copy in copies:
+        copy.wait()
 
 
 def on_device(sections, parts, rhs, inverse, diag, lower, upper, halo, low_index, up_index, halo_index):
@@ -447,7 +456,7 @@
     hbm = pl.BlockSpec(memory_space=pl.ANY)
     vmem = pl.BlockSpec(memory_space=pltpu.VMEM)
     dma = pltpu.SemaphoreType.DMA
-    return pl.pallas_call(
+    solved, product = pl.pallas_call(
         functools.partial(kernel, sections, parts),
         out_shape=(
             pltpu.VMEM(rhs.shape, F32),
@@ -482,8 +491,8 @@
             dma((9,)),
             dma((2,)),
             dma((2,)),
-            dma((1,)),
-            dma((chips, 2)),
+            dma((2,)),
+            dma((chips, 2, 2)),
             dma((chips, 2, 2)),
             dma((2,)),
             dma((1,)),
@@ -494,6 +503,16 @@
         compiler_params=pltpu.CompilerParams(collective_id=0, has_side_effects=True),
         name="block_ilu_apply",
     )(low_index.T, up_index.T, halo_index.T, rhs, inverse, diag, lower, upper, halo)
+    solved = pltpu.with_memory_space_constraint(solved, pltpu.VMEM)
+    product = pltpu.with_memory_space_constraint(product, pltpu.VMEM)
+    return pl.pallas_call(
+        store,
+        out_shape=(jax.ShapeDtypeStruct(rhs.shape, F32),) * 2,
+        in_specs=[vmem] * 2,
+        out_specs=(hbm, hbm),
+        scratch_shapes=[dma((2,))],
+        name="store_outputs",
+    )(solved, product)
 
 
 def solution(mesh):

time: 27.6 us -> 26.1 us (0.946)
  local copies, waits for them, and re-layouts: 1.31 us -> 0 us
    unnamed x2 -> x0, local copies, waits for them, and re-layouts: 1.31 us -> none
    pallas_call x1, Pallas kernels: 25.5 us -> 24.6 us  [on_device(): pl.pallas_call(functools.partial(kernel, sections, parts), out_shape=(plt...]
    pallas_call x0 -> x1, Pallas kernels: none -> 0.72 us  [on_device(): pl.pallas_call(store, out_shape=(jax.ShapeDtypeStruct(rhs.shape, F32),) *...]
where the time goes in v6:
time: 26.1 us; the launch traced here: 25.9 us
  Pallas kernels  25.3 us (97%)
  between operations  0.64 us (2%)
    pallas_call x1, Pallas kernels, on_device(): pl.pallas_call(functools.partial(kernel, sections, parts), out_shape=(plt...  24.6 us
    pallas_call x1, Pallas kernels, on_device(): pl.pallas_call(store, out_shape=(jax.ShapeDtypeStruct(rhs.shape, F32),) *...  0.72 us

profile of v6, /device:TPU:206, one launch (start us, length us, event | category | flops | bytes accessed | tf_op | source)
XLA Modules:
  0.0 25.9 jit_solution(4278375650636687450)
XLA Ops:
  0.6 24.6 %block_ilu_apply.1 = (f32[8,32,128]{2,1,0:T(8,128)S(1)}, f32[8,32,128]{2,1,0:T(8,128)S(1)}) custom-call(s32[3,8]{1,0:T(4,128)} %bitcast.3, s32[3,8]{1,0:T(4,128)} %bitcast.4, s32[2,8]{1,0:T(2,128)} %bitcast.5, f32[8,32,128]{2,1,0:T(8,128)} %rhs_hbm.1, bf16[8,128,128]{2,1,0:T(8,128)(2,1)} %inverse_hbm.1, bf16[8,128,128]{2,1,0:T(8,128)(2,1)} %diag_hbm.1, ...), custom_call_target="tpu_custom_call" | custom-call | tf_op jit(solution)/shard_map/block_ilu_apply/pallas_call | solution.py:459
  25.2 0.7 %store_outputs.1 = (f32[8,32,128]{2,1,0:T(8,128)}, f32[8,32,128]{2,1,0:T(8,128)}) custom-call(f32[8,32,128]{2,1,0:T(8,128)S(1)} %get-tuple-element.4.solved, f32[8,32,128]{2,1,0:T(8,128)S(1)} %get-tuple-element.5.product), custom_call_target="tpu_custom_call" | custom-call | tf_op jit(solution)/shard_map/store_outputs/pallas_call | solution.py:508

commit v7 on v6

--- a/solution.py
+++ b/solution.py
@@ -110,9 +110,10 @@
     for place, (source, target) in enumerate(
         (
             (lower_index_hbm, lower_index),
-            (lower_hbm, lower),
+            (lower_hbm.at[pl.ds(0, 3)], lower.at[pl.ds(0, 3)]),
             (inverse_hbm, inverse),
             (rhs_hbm, rhs),
+            (lower_hbm.at[pl.ds(3, 5)], lower.at[pl.ds(3, 5)]),
             (upper_index_hbm, upper_index),
             (upper_hbm, upper),
             (halo_index_hbm, halo_index),
@@ -174,6 +175,8 @@
     for copy in loads[:4]:
         copy.wait()
     for k in range(ROWS):
+        if k == 3:
+            loads[4].wait()
         folded = dot(lower[k].reshape(3 * BLK, BLK), inverse[k])
         base = jnp.concatenate([folded[:BLK] * -has_before, dot(rhs[k], inverse[k])], axis=0)
         slots = [jnp.where(lower_index[m, k] == k, ROWS, lower_index[m, k]) for m in (1, 2)]
@@ -200,7 +203,7 @@
     pair_back = pair_copy(1, AFFINE, ELEMENT)
     pair_onward.start()
 
-    for copy in loads[4:6]:
+    for copy in loads[5:7]:
         copy.wait()
     for k in range(ROWS - 1, -1, -1):
         folded = dot(upper[k].reshape(3 * BLK, BLK), inverse[k])
@@ -294,46 +297,61 @@
             for copy in result_copies(kind, target):
                 copy.start()
 
-        order = sorted(range(1, chips), key=lambda c: min(c, chips - c))
-        for origin in order:
-            take(origin, 0)
+        def known(origin):
+            values = part_of(origin, AFFINE + BLK, NRHS).astype(F32)
+            return values + dot(inflows[origin], part_of(origin, AFFINE, BLK))
+
+        def first_of(origin):
+            sources = jnp.concatenate([inflows[origin], outflows[origin]], axis=1)
+            maps = [part_of(origin, AFFINE, BLK), part_of(origin, 2 * AFFINE, BLK)]
+            values = part_of(origin, AFFINE + BLK, NRHS).astype(F32)
+            return values + dot(sources, jnp.concatenate(maps, axis=0))
+
         running = None
-        for origin in range(chips - 1):
+        for origin in range(middle_chip):
+            if origin:
+                take(origin, 0)
             running = onward(origin, running)
             give(0, origin + 1, running)
-        for origin in order[:-1]:
-            take(origin, 1)
-        runs = [None] * chips
-        runs[-1] = part_of(chips - 1, AFFINE, AFFINE)
-        for origin in range(chips - 2, middle_chip, -1):
-            runs[origin] = joined_back(
-                part_of(origin, 0, AFFINE), part_of(origin, AFFINE, WIDE), runs[origin + 1]
-            )
-        for origin in range(middle_chip, chips - 1):
-            beyond_run = runs[origin + 1]
-            outflow = beyond_run[BLK:].astype(F32) + dot(inflows[origin + 1], beyond_run[:BLK])
-            give(1, origin, outflow)
+        nearer = middle_chip - 1
         shifts = [None] * chips
         gains = [None] * chips
-        for origin in range(middle_chip - 1, 0, -1):
-            shift = part_of(origin, AFFINE + BLK, NRHS).astype(F32) + dot(
-                inflows[origin], part_of(origin, AFFINE, BLK)
-            )
+        for origin in range(1, nearer):
+            take(origin, 1)
+        for origin in range(nearer - 1, 0, -1):
             gain = part_of(origin, 2 * AFFINE, BLK)
-            if origin < middle_chip - 1:
+            shift = known(origin)
+            if origin < nearer - 1:
                 shift = shift + dot(shifts[origin + 1], gain)
                 gain = dot(gains[origin + 1], gain).astype(BF16)
             shifts[origin], gains[origin] = shift, gain
+        for origin in range(chips - 1, middle_chip + 1, -1):
+            take(origin, 0)
+            take(origin, 1)
+        if middle_chip + 1 < chips - 1:
+            take(middle_chip + 1, 0)
+        take(middle_chip, 0)
+        for origin in range(middle_chip, chips - 1):
+            running = onward(origin, running)
+            give(0, origin + 1, running)
+        for origin in range(chips - 1, middle_chip, -1):
+            if origin == middle_chip + 1:
+                take(origin, 1)
+            give(1, origin - 1, first_of(origin) if origin < chips - 1 else known(origin))
+        take(nearer, 1)
+        shift = known(nearer)
+        gain = part_of(nearer, 2 * AFFINE, BLK)
+        ahead = jnp.concatenate([gain, shift.astype(BF16)], axis=0)
+        for origin in range(1, nearer):
+            through = dot(ahead, gains[origin])
+            gains[origin] = through[:BLK].astype(BF16)
+            shifts[origin] = shifts[origin] + through[BLK:]
+        shifts[nearer], gains[nearer] = shift, gain
 
         take(middle_chip, 1)
-        first = part_of(middle_chip, AFFINE + BLK, NRHS).astype(F32) + dot(
-            jnp.concatenate([inflows[middle_chip], outflows[middle_chip]], axis=1),
-            jnp.concatenate(
-                [part_of(middle_chip, AFFINE, BLK), part_of(middle_chip, 2 * AFFINE, BLK)], axis=0
-            ),
-        )
-        give(1, middle_chip - 1, first)
-        for origin in range(middle_chip - 1, 0, -1):
+        first = first_of(middle_chip)
+        give(1, nearer, first)
+        for origin in range(nearer, 0, -1):
             give(1, origin - 1, shifts[origin] + dot(first, gains[origin]))
         got[1] = outflows[0]
 
@@ -356,12 +374,6 @@
     inflow = jnp.where(core == 0, inflow, middle)
     outflow = jnp.where(core == 0, centre, outflow)
     flows = jnp.concatenate([inflow, outflow], axis=1).astype(BF16)
-    for k in range(ROWS):
-        response = jnp.concatenate([bwd[k, :BLK], bwd[k, AFFINE:]], axis=0)
-        solved = bwd_values[k] + dot(flows, response)
-        solution_ref[k] = solved
-        rows[k] = solved.astype(BF16)
-
     rim_copies = [
         pltpu.make_async_remote_copy(
             src_ref=rows.at[pl.ds(ROWS - RIM, RIM)],
@@ -380,19 +392,23 @@
             device_id_type=MESH,
         ),
     ]
-    @pl.when(part < parts - 1)
-    def _():
-        rim_copies[0].start()
-
-    @pl.when(part > 0)
-    def _():
-        rim_copies[1].start()
+    def solve_rows(low, high):
+        for k in range(low, high):
+            response = jnp.concatenate([bwd[k, :BLK], bwd[k, AFFINE:]], axis=0)
+            solved = bwd_values[k] + dot(flows, response)
+            solution_ref[k] = solved
+            rows[k] = solved.astype(BF16)
+
+    solve_rows(0, RIM)
+    pl.when(part > 0)(rim_copies[1].start)
+    solve_rows(RIM, ROWS)
+    pl.when(part < parts - 1)(rim_copies[0].start)
 
     last_copy.wait_recv()
     edges_before = (inflow - dot(rows[0], last_in[...])) * has_before
     edges = jnp.stack([edges_before, outflow * has_after]).astype(BF16)
     rows[pl.ds(ROWS, 2)] = edges
-    for copy in loads[6:]:
+    for copy in loads[7:]:
         copy.wait()
     totals = []
     for k in range(ROWS):
@@ -488,7 +504,7 @@
             pltpu.VMEM((BLK, BLK), BF16),
             pltpu.VMEM((ROWS + 2, NRHS, BLK), BF16),
             pltpu.VMEM((2 * RIM, NRHS, BLK), BF16),
-            dma((9,)),
+            dma((10,)),
             dma((2,)),
             dma((2,)),
             dma((2,)),

time: 26.1 us -> 25.9 us (level)
  no operation moved by 1% of the time
where the time goes in v7:
time: 25.9 us; the launch traced here: 25.8 us
  Pallas kernels  25.2 us (97%)
  between operations  0.64 us (2%)
    pallas_call x1, Pallas kernels, on_device(): pl.pallas_call(functools.partial(kernel, sections, parts), out_shape=(plt...  24.4 us
    pallas_call x1, Pallas kernels, on_device(): pl.pallas_call(store, out_shape=(jax.ShapeDtypeStruct(rhs.shape, F32),) *...  0.72 us

profile of v7, /device:TPU:206, one launch (start us, length us, event | category | flops | bytes accessed | tf_op | source)
XLA Modules:
  0.0 25.8 jit_solution(16865965704702392661)
XLA Ops:
  0.6 24.4 %block_ilu_apply.1 = (f32[8,32,128]{2,1,0:T(8,128)S(1)}, f32[8,32,128]{2,1,0:T(8,128)S(1)}) custom-call(s32[3,8]{1,0:T(4,128)} %bitcast.3, s32[3,8]{1,0:T(4,128)} %bitcast.4, s32[2,8]{1,0:T(2,128)} %bitcast.5, f32[8,32,128]{2,1,0:T(8,128)} %rhs_hbm.1, bf16[8,128,128]{2,1,0:T(8,128)(2,1)} %inverse_hbm.1, bf16[8,128,128]{2,1,0:T(8,128)(2,1)} %diag_hbm.1, ...), custom_call_target="tpu_custom_call" | custom-call | tf_op jit(solution)/shard_map/block_ilu_apply/pallas_call | solution.py:475
  25.1 0.7 %store_outputs.1 = (f32[8,32,128]{2,1,0:T(8,128)}, f32[8,32,128]{2,1,0:T(8,128)}) custom-call(f32[8,32,128]{2,1,0:T(8,128)S(1)} %get-tuple-element.4.solved, f32[8,32,128]{2,1,0:T(8,128)S(1)} %get-tuple-element.5.product), custom_call_target="tpu_custom_call" | custom-call | tf_op jit(solution)/shard_map/store_outputs/pallas_call | solution.py:524

commit v8 on v7

--- a/solution.py
+++ b/solution.py
@@ -155,6 +155,10 @@
     def _():
         rim[pl.ds(RIM, RIM)] = jnp.zeros((RIM, NRHS, BLK), BF16)
 
+    @pl.when(section == 0)
+    def _():
+        last_in[...] = jnp.zeros((BLK, BLK), BF16)
+
     @pl.when(chip == 0)
     def _():
         got[0] = jnp.zeros((NRHS, BLK), BF16)
@@ -217,7 +221,7 @@
                 device_id=following,
                 device_id_type=MESH,
             )
-            last_copy.start()
+            pl.when(section < sections - 1)(last_copy.start)
         base = jnp.concatenate([fwd_wide[k], folded[:BLK] * -has_after], axis=0)
         slots = [jnp.where(upper_index[m, k] == k, ROWS, upper_index[m, k]) for m in (1, 2)]
         sources = jnp.concatenate([bwd[slot] for slot in slots], axis=1)
@@ -404,7 +408,7 @@
     solve_rows(RIM, ROWS)
     pl.when(part < parts - 1)(rim_copies[0].start)
 
-    last_copy.wait_recv()
+    pl.when(section > 0)(last_copy.wait_recv)
     edges_before = (inflow - dot(rows[0], last_in[...])) * has_before
     edges = jnp.stack([edges_before, outflow * has_after]).astype(BF16)
     rows[pl.ds(ROWS, 2)] = edges
@@ -435,7 +439,7 @@
 
     pair_onward.wait_send()
     pair_back.wait_send()
-    last_copy.wait_send()
+    pl.when(section < sections - 1)(last_copy.wait_send)
 
     @pl.when(part < parts - 1)
     def _():

time: 25.9 us -> 25.9 us (level)
  no operation moved by 1% of the time
where the time goes in v8:
time: 25.9 us; the launch traced here: 25.8 us
  Pallas kernels  25.2 us (97%)
  between operations  0.64 us (2%)
    pallas_call x1, Pallas kernels, on_device(): pl.pallas_call(functools.partial(kernel, sections, parts), out_shape=(plt...  24.4 us
    pallas_call x1, Pallas kernels, on_device(): pl.pallas_call(store, out_shape=(jax.ShapeDtypeStruct(rhs.shape, F32),) *...  0.72 us

profile of v8, /device:TPU:206, one launch (start us, length us, event | category | flops | bytes accessed | tf_op | source)
XLA Modules:
  0.0 25.8 jit_solution(16551423772937902948)
XLA Ops:
  0.6 24.4 %block_ilu_apply.1 = (f32[8,32,128]{2,1,0:T(8,128)S(1)}, f32[8,32,128]{2,1,0:T(8,128)S(1)}) custom-call(s32[3,8]{1,0:T(4,128)} %bitcast.3, s32[3,8]{1,0:T(4,128)} %bitcast.4, s32[2,8]{1,0:T(2,128)} %bitcast.5, f32[8,32,128]{2,1,0:T(8,128)} %rhs_hbm.1, bf16[8,128,128]{2,1,0:T(8,128)(2,1)} %inverse_hbm.1, bf16[8,128,128]{2,1,0:T(8,128)(2,1)} %diag_hbm.1, ...), custom_call_target="tpu_custom_call" | custom-call | tf_op jit(solution)/shard_map/block_ilu_apply/pallas_call | solution.py:479
  25.1 0.7 %store_outputs.1 = (f32[8,32,128]{2,1,0:T(8,128)}, f32[8,32,128]{2,1,0:T(8,128)}) custom-call(f32[8,32,128]{2,1,0:T(8,128)S(1)} %get-tuple-element.4.solved, f32[8,32,128]{2,1,0:T(8,128)S(1)} %get-tuple-element.5.product), custom_call_target="tpu_custom_call" | custom-call | tf_op jit(solution)/shard_map/store_outputs/pallas_call | solution.py:528
